TPU v7x, 256 devices: a whole 4x4x8 slice. The times are simulated.
256 devices in a mesh: atom: 128 (over z, y, x), wave: 2 (over core).
Axes of the slice: x: 4, y: 4, z: 8, core: 2. Of those that a mesh axis runs over, the one named last changes fastest.
Arguments:
- positions: float32 [3, 32768], P(None, ('atom', 'wave')), may hold values from 0 to 1
- counts: int32 [256], P(('atom', 'wave')), may hold values from 16 to 128, as said below
- feats: bfloat16 [32768, 256], P(('atom', 'wave')), may hold values from -6 to 6
- waves: int32 [3, 8192], P(None, 'wave'), may hold values from -12 to 12
- wave_filter: bfloat16 [8192, 256], P('wave'), may hold values from -5 to 5
- mixing: float32 [256, 256], replicated, may hold values from -0.375 to 0.375
- gain: float32 [256], replicated, may hold values from 0.1 to 1.9
- w_in: bfloat16 [256, 1024], replicated, may hold values from -0.375 to 0.375
- w_out: bfloat16 [1024, 256], replicated, may hold values from -0.1875 to 0.1875
Outputs:
- updated: bfloat16 [32768, 256], P(('atom', 'wave'))
Inputs may be any that keep to these rules, and one draw needn't show every extreme that they name: `counts`: each block of 128 slots holds 16 to 128 live atoms at its start; every even-numbered block is full.
All inputs are finite; a program needn't handle non-finite values.
Results may differ from a plain program's by a relative error of at most 0.0055.
Values may be sent and summed in bfloat16 or wider, within the bound.
No kernel may reach another device: no remote copies, remote signals or barrier semaphores. Data moves between devices by JAX's collectives and lax.ppermute only.
A program may use at most 128 MiB of HBM per device.

v0:
```python
import math

import jax
import jax.numpy as jnp
from jax import lax
from jax.experimental import pallas as pl
from jax.experimental.pallas import tpu as pltpu
from jax.sharding import Mesh
from jax.sharding import PartitionSpec as P

bf16 = jnp.bfloat16
f32 = jnp.float32

NZ, NY, NX, NC = 8, 4, 4, 2
NYX = NY * NX
HALF = NZ // 2


ROOT2 = math.sqrt(2.0)
SIN_C = (
    3.1415926520468305,
    -5.167710734303894,
    2.550084223872135,
    -0.5983094608569061,
    0.07765872505863924,
)
COS_C = (
    0.9999999946405678,
    -4.934795092504032,
    4.058434665884265,
    -1.3319399977127386,
    0.21969398917152252,
)
MAGIC = 1.5 * 2.0**23


def poly(coefs, w):
    acc = coefs[-1] * ROOT2
    for c in coefs[-2::-1]:
        acc = acc * w + c * ROOT2
    return acc


def cos_sin(turns):
    u = turns - ((turns + MAGIC) - MAGIC)
    w = u * u
    s = u * poly(SIN_C, w)
    c = poly(COS_C, w)
    return 1.0 - s * s, s * c


VMEM = pl.BlockSpec(memory_space=pltpu.VMEM)
SMALL = pltpu.CompilerParams(vmem_limit_bytes=16 << 20)


def on_chip(*values):
    return [pltpu.with_memory_space_constraint(v, pltpu.VMEM) for v in values]


def in_hbm(*values):
    return [pltpu.with_memory_space_constraint(v, pltpu.HBM) for v in values]


def pack_kernel(count_ref, _z, _slot, pos_ref, feats_ref, waves_ref, filt_ref, out_ref, waves_out, filt_out):
    rows = feats_ref.shape[0]
    waves = waves_ref[...].astype(f32)
    waves_out[...] = jnp.concatenate(
        [waves, waves, waves, jnp.zeros((7, waves.shape[1]), f32)], axis=0
    ).astype(bf16)
    filt_out[...] = filt_ref[...]
    slot = lax.broadcasted_iota(jnp.int32, feats_ref.shape, 0)
    live = slot < count_ref[0]
    feats = feats_ref[...].astype(f32)
    out_ref[0:rows, :] = jnp.where(live, feats, 0.0).astype(bf16)
    pos = pos_ref[...]
    hi = pos.astype(bf16).astype(f32)
    rest = pos - hi
    mid = rest.astype(bf16).astype(f32)
    low = rest - mid
    n = pos.shape[1]
    tail = jnp.concatenate([hi, mid, low, jnp.zeros((7, n), f32)], axis=0)
    out_ref[rows : rows + 16, :] = jnp.concatenate(
        [tail, jnp.zeros((16, feats.shape[1] - n), f32)], axis=1
    ).astype(bf16)


def pack(counts, z, slot, positions, feats, waves, wave_filter, share, own):
    rows, width = feats.shape

    def whole(v):
        return pl.BlockSpec(v.shape, lambda i, c, z, s: (0, 0))

    return pl.pallas_call(
        pack_kernel,
        grid_spec=pltpu.PrefetchScalarGridSpec(
            num_scalar_prefetch=3,
            grid=(1,),
            in_specs=[
                whole(positions),
                whole(feats),
                pl.BlockSpec((3, share), lambda i, c, z, s: (0, z[0])),
                pl.BlockSpec((own, width), lambda i, c, z, s: (s[0], 0)),
            ],
            out_specs=(
                pl.BlockSpec((rows + 16, width), lambda i, c, z, s: (0, 0)),
                pl.BlockSpec((16, share), lambda i, c, z, s: (0, 0)),
                pl.BlockSpec((own, width), lambda i, c, z, s: (0, 0)),
            ),
        ),
        out_shape=(
            jax.ShapeDtypeStruct((rows + 16, width), bf16),
            jax.ShapeDtypeStruct((16, share), bf16),
            jax.ShapeDtypeStruct((own, width), bf16),
        ),
        compiler_params=SMALL,
        name="pack_atoms",
    )(counts, z[None], slot[None], *in_hbm(positions, feats, waves, wave_filter))


OWN = 32
EXTRA = 16


def load_blocks(block_refs, layout, feats, coords):
    n = coords.shape[1] // len(layout)
    for j, (source, k) in enumerate(layout):
        block = block_refs[source]
        at = k * (n + EXTRA)
        if feats is not None:
            feats[j * n : (j + 1) * n, :] = block[at : at + n, :]
        coords[:, j * n : (j + 1) * n] = block[at + n : at + n + EXTRA, 0:n]


def fill_tile(waves_ref, coords, turns, tile_ref):
    rows, _ = turns.shape
    turns[...] = jnp.dot(
        waves_ref[...].astype(f32).T.astype(bf16), coords[...], preferred_element_type=f32
    )

    def step(i, carry):
        for h in range(0, OWN, 16):
            at = pl.ds(pl.multiple_of(i * OWN + h, 16), 16)
            to_cos = pl.ds(pl.multiple_of(i * 2 * OWN + h, 16), 16)
            to_sin = pl.ds(pl.multiple_of(i * 2 * OWN + OWN + h, 16), 16)
            c, s = cos_sin(turns[at, :])
            tile_ref[to_cos, :] = c.astype(bf16)
            tile_ref[to_sin, :] = s.astype(bf16)
        return carry

    lax.fori_loop(0, rows // OWN, step, 0, unroll=2)


def early_tiles(both_waves, blocks, layout):
    rows = both_waves[0].shape[1]
    n = blocks[0].shape[0] - EXTRA
    atoms = n * len(layout)
    nb = len(blocks)

    def kernel(*refs):
        out_a, out_b, coords, turns = refs[2 + nb :]
        load_blocks(refs[2 : 2 + nb], layout, None, coords)
        fill_tile(refs[0], coords, turns, out_a)
        fill_tile(refs[1], coords, turns, out_b)

    return pl.pallas_call(
        kernel,
        out_shape=(pltpu.VMEM((2 * rows, atoms), bf16),) * 2,
        in_specs=[VMEM] * (2 + nb),
        out_specs=(VMEM, VMEM),
        scratch_shapes=[pltpu.VMEM((EXTRA, atoms), bf16), pltpu.VMEM((rows, atoms), f32)],
        compiler_params=SMALL,
        cost_estimate=pl.CostEstimate(
            flops=1024 * rows * atoms, transcendentals=0, bytes_accessed=8 * rows * atoms
        ),
        name="early_tiles",
    )(*on_chip(*both_waves, *blocks))


def factors(waves9, tile, early, early_layout, late, late_layout, dtype):
    rows = waves9.shape[1]
    width = early[0].shape[1]
    n = early[0].shape[0] - EXTRA
    atoms = n * len(late_layout)
    ready = n * len(early_layout)
    groups = rows // OWN
    ne, nl = len(early), len(late)

    def kernel(*refs):
        waves_ref, ready_ref = refs[:2]
        early_refs = refs[2 : 2 + ne]
        late_refs = refs[2 + ne : 2 + ne + nl]
        out_ref, tile_ref, feats_a, feats_b, coords_a, coords_b, turns = refs[2 + ne + nl :]
        load_blocks(early_refs, early_layout, feats_a, coords_a)
        load_blocks(late_refs, late_layout, feats_b, coords_b)
        fill_tile(waves_ref, coords_b, turns, tile_ref)
        summed = jnp.dot(ready_ref[...], feats_a[...], preferred_element_type=f32)
        summed = summed + jnp.dot(tile_ref[...], feats_b[...], preferred_element_type=f32)
        out_ref[...] = summed.astype(dtype).reshape(groups, 2, OWN, width)

    return pl.pallas_call(
        kernel,
        out_shape=(
            pltpu.VMEM((groups, 2, OWN, width), dtype),
            pltpu.VMEM((2 * rows, atoms), bf16),
        ),
        in_specs=[VMEM] * (2 + ne + nl),
        out_specs=(VMEM, VMEM),
        scratch_shapes=[
            pltpu.VMEM((ready, width), bf16),
            pltpu.VMEM((atoms, width), bf16),
            pltpu.VMEM((EXTRA, ready), bf16),
            pltpu.VMEM((EXTRA, atoms), bf16),
            pltpu.VMEM((rows, atoms), f32),
        ],
        compiler_params=SMALL,
        cost_estimate=pl.CostEstimate(
            flops=8 * rows * atoms * width, transcendentals=0, bytes_accessed=8 * rows * atoms
        ),
        name="structure_factors",
    )(*on_chip(waves9, tile, *early, *late))


def filter_kernel(arrived_ref, filt_ref, mix_ref, out_ref, *, scale):
    n = arrived_ref.shape[0]
    total = arrived_ref[0].astype(f32)
    for j in range(1, n):
        total = total + arrived_ref[j].astype(f32)
    filt = filt_ref[...].astype(f32)
    both = jnp.concatenate([total[0] * scale * filt, total[1] * scale * filt], axis=0)
    mixed = jnp.dot(
        both, mix_ref[...], precision=lax.Precision.HIGHEST, preferred_element_type=f32
    ).astype(bf16)
    rows = filt.shape[0]
    for j in range(n):
        out_ref[j, 0] = mixed[:rows]
        out_ref[j, 1] = mixed[rows:]


def filter_mix(arrived, filt, mixing, scale):
    return pl.pallas_call(
        lambda *refs: filter_kernel(*refs, scale=scale),
        out_shape=pltpu.VMEM(arrived.shape, bf16),
        in_specs=[VMEM] * 3,
        out_specs=VMEM,
        compiler_params=SMALL,
        name="filter_mix",
    )(*on_chip(arrived, filt, mixing))


def fields(tiles, halves, outs, after=()):
    owners, two, own, width = halves[0].shape
    half = owners * two * own
    n = 128
    wanted = [place for places, _ in outs for place in places]
    first = min(j for _, j in wanted)
    last = max(j for _, j in wanted) + 1

    def kernel(*refs):
        tile_refs, half_refs = refs[:4], refs[4:6]
        out_refs = refs[6 + len(after) :]
        left = [f[...].reshape(half, width).T for f in half_refs]
        got = []
        for t in range(2):
            field = None
            for h in range(2):
                part = jnp.dot(
                    left[h],
                    tile_refs[2 * h + t][:, first * n : last * n],
                    preferred_element_type=f32,
                )
                field = part if field is None else field + part
            got.append(field)
        for out, (places, dtype) in zip(out_refs, outs):
            for k, (t, j) in enumerate(places):
                at = (j - first) * n
                out[k] = got[t][:, at : at + n].astype(dtype)

    return pl.pallas_call(
        kernel,
        out_shape=tuple(pltpu.VMEM((len(places), width, n), d) for places, d in outs),
        in_specs=[VMEM] * 6 + [pl.BlockSpec(memory_space=pl.ANY)] * len(after),
        out_specs=(VMEM,) * len(outs),
        compiler_params=SMALL,
        cost_estimate=pl.CostEstimate(
            flops=4 * half * width * n * len(wanted),
            transcendentals=0,
            bytes_accessed=4 * half * n * len(wanted),
        ),
        name="wave_fields",
    )(*on_chip(*tiles, *halves), *after)


def update_kernel(count_ref, *refs, scale):
    part_refs = refs[:-5]
    feats_ref, gain_ref, win_ref, wout_ref, out_ref = refs[-5:]
    total = part_refs[0][0].astype(f32)
    for part in part_refs[1:]:
        total = total + part[0].astype(f32)
    state = feats_ref[...].astype(f32) + (total * scale).T
    meansq = jnp.mean(state * state, axis=1, keepdims=True)
    normed = (state * lax.rsqrt(meansq + 1e-06) * gain_ref[...]).astype(bf16)
    v = jnp.dot(normed, win_ref[...], preferred_element_type=f32)
    hidden = (v / (1.0 + jnp.exp(-v))).astype(bf16)
    result = state + jnp.dot(hidden, wout_ref[...], preferred_element_type=f32)
    slot = lax.broadcasted_iota(jnp.int32, result.shape, 0)
    out_ref[...] = jnp.where(slot < count_ref[0], result, 0.0).astype(bf16)


def update(counts, parts, feats, gain, w_in, w_out, scale):
    return pl.pallas_call(
        lambda *refs: update_kernel(*refs, scale=scale),
        out_shape=jax.ShapeDtypeStruct(feats.shape, bf16),
        in_specs=[pl.BlockSpec(memory_space=pltpu.SMEM)] + [VMEM] * (len(parts) + 4),
        out_specs=VMEM,
        compiler_params=SMALL,
        name="update_atoms",
    )(counts, *on_chip(*parts, feats, gain[None, :], w_in, w_out))


def layer(positions, counts, feats, waves, wave_filter, mixing, gain, w_in, w_out):
    kw = waves.shape[1]
    share = kw // NZ
    own_waves = share // NYX
    atoms_all = feats.shape[0] * NZ * NYX * NC
    kwaves_all = kw * NC
    z = lax.axis_index("z")
    yx = lax.axis_index("y") * NX + lax.axis_index("x")
    swap = [(0, 1), (1, 0)]

    def partner(v):
        return lax.ppermute(v, "core", swap)

    def shift(v, d):
        return lax.ppermute(v, "z", [(i, (i + d) % NZ) for i in range(NZ)]) if d else v

    def exchange(v):
        return lax.all_to_all(v, ("y", "x"), 0, 0, tiled=True)

    block, mine, filt = pack(
        counts, z, z * NYX + yx, positions, feats, waves, wave_filter, share, own_waves
    )
    other = partner(mine)
    opposite = shift(block, HALF)
    ahead = shift(block, -2)
    behind = shift(block, 2)
    pair = jnp.concatenate([block, opposite], axis=0)
    near_behind = shift(pair, 1)
    near_ahead = shift(pair, -1)
    early = [ahead, behind, opposite, block]
    early_layout = [(0, 0), (1, 0), (2, 0), (3, 0)]
    late = [near_behind, near_ahead]
    late_layout = [(0, 1), (1, 1), (1, 0), (0, 0)]
    ready_other, ready_mine = early_tiles([other, mine], early, early_layout)
    sent, tile_other = factors(other, ready_other, early, early_layout, late, late_layout, bf16)
    arrived = partner(sent)
    kept, tile_mine = factors(mine, ready_mine, early, early_layout, late, late_layout, f32)
    summed = exchange((kept + arrived.astype(f32)).astype(bf16))
    spread = filter_mix(summed, filt, mixing, 1.0 / math.sqrt(atoms_all))
    filtered = exchange(spread)
    halves = (partner(filtered), filtered)

    tiles = (ready_other, tile_other, ready_mine, tile_mine)
    to_ahead, to_behind = fields(
        tiles, halves, [([(0, 0), (1, 0)], bf16), ([(0, 1), (1, 1)], bf16)]
    )
    far, own, one_ahead, one_behind = fields(
        tiles,
        halves,
        [([(0, 2)], bf16), ([(0, 3)], f32), ([(1, 2)], f32), ([(1, 3)], f32)],
        (to_ahead,),
    )
    from_behind = shift(to_ahead, 2)
    from_ahead = shift(to_behind, -2)
    opposite = shift(far, HALF)
    one_ahead = (one_ahead + from_behind[1:].astype(f32)).astype(bf16)
    one_behind = (one_behind + from_ahead[1:].astype(f32)).astype(bf16)
    near_behind = shift(one_ahead, 1)
    near_ahead = shift(one_behind, -1)
    parts = [own, from_ahead, from_behind, opposite, near_behind, near_ahead]
    return update(counts, parts, feats, gain, w_in, w_out, 1.0 / math.sqrt(kwaves_all))


def solution(mesh):
    fine = Mesh(mesh.devices.reshape(NZ, NY, NX, NC), ("z", "y", "x", "core"))
    every = ("z", "y", "x", "core")
    return jax.shard_map(
        layer,
        mesh=fine,
        in_specs=(
            P(None, every),
            P(every),
            P(every, None),
            P(None, "core"),
            P("core", None),
            P(),
            P(),
            P(),
            P(),
        ),
        out_specs=P(every, None),
        check_vma=False,
    )
```

profile of v0, /device:TPU:1, one launch (start us, length us, event | category | flops | bytes accessed | tf_op | source)
XLA Modules:
  0.0 86.1 jit_solution(14102276444231337688)
XLA Ops:
  0.7 0.9 %pack_atoms.1 = (bf16[144,256]{1,0:T(8,128)(2,1)S(1)}, bf16[16,512]{1,0:T(8,128)(2,1)S(1)}, bf16[32,256]{1,0:T(8,128)(2,1)S(1)}) custom-call(s32[1]{0:T(128)S(6)} %copy.11.count_ref.refs_0_, s32[1]{0:T(128)} %bitcast._z, s32[1]{0:T(128)} %bitcast.1._slot, f32[3,128]{1,0:T(4,128)} %pos_ref.1, bf16[128,256]{1,0:T(8,128)(2,1)} %refs_7_.1, s32[3,4096]{1,0:T(4,128)} %waves_ref.1, ...), custom_call_target="tpu_custom_call" | custom-call | tf_op jit(solution)/shard_map/pack_atoms/pallas_call | solution.py:93
  1.5 7.8 %collective-permute-start.3 = (bf16[144,256]{1,0:T(8,128)(2,1)S(1)}, bf16[144,256]{1,0:T(8,128)(2,1)S(1)}, u32[]{:S(2)}, u32[]{:S(2)}) collective-permute-start(bf16[144,256]{1,0:T(8,128)(2,1)S(1)} %get-tuple-element.21.refs_5_), channel_id=1, source_target_pairs={{0,128},{32,160},{64,192},{96,224},{128,0},{160,32},{192,64},{224,... | collective-permute-start | bytes 221192 | tf_op jit(solution)/shard_map/ppermute | solution.py:334
  9.3 1.8 %collective-permute-done.3.refs_4_ = bf16[144,256]{1,0:T(8,128)(2,1)S(1)} collective-permute-done((bf16[144,256]{1,0:T(8,128)(2,1)S(1)}, bf16[144,256]{1,0:T(8,128)(2,1)S(1)}, u32[]{:S(2)}, u32[]{:S(2)}) %collective-permute-start.3) | collective-permute-done | bytes 73760 | tf_op jit(solution)/shard_map/ppermute | solution.py:334
  11.2 4.8 %collective-permute-start.5 = (bf16[288,256]{1,0:T(8,128)(2,1)S(1)}, bf16[288,256]{1,0:T(8,128)(2,1)S(1)}, u32[]{:S(2)}, u32[]{:S(2)}) collective-permute-start(bf16[288,256]{1,0:T(8,128)(2,1)S(1)} %constant_dynamic-update-slice_fusion), channel_id=1, source_target_pairs={{0,224},{32,0},{64,32},{96,64},{128,96},{160,128},{192,160},{224,1... | collective-permute-start | bytes 442376 | tf_op jit(solution)/shard_map/ppermute | solution.py:334
  16.0 0.0 collective-permute-start.4
  16.0 0.0 collective-permute-start.2
  16.0 3.6 %collective-permute-start.1 = (bf16[144,256]{1,0:T(8,128)(2,1)S(1)}, bf16[144,256]{1,0:T(8,128)(2,1)S(1)}, u32[]{:S(2)}, u32[]{:S(2)}) collective-permute-start(bf16[144,256]{1,0:T(8,128)(2,1)S(1)} %get-tuple-element.21.refs_5_), channel_id=1, source_target_pairs={{0,192},{32,224},{64,0},{96,32},{128,64},{160,96},{192,128},{224,1... | collective-permute-start | bytes 221192 | tf_op jit(solution)/shard_map/ppermute | solution.py:334
  19.6 2.0 %collective-permute-start = (bf16[16,512]{1,0:T(8,128)(2,1)S(1)}, bf16[16,512]{1,0:T(8,128)(2,1)S(1)}, u32[]{:S(2)}, u32[]{:S(2)}) collective-permute-start(bf16[16,512]{1,0:T(8,128)(2,1)S(1)} %get-tuple-element.20.refs_1_.refs_0_), channel_id=1, source_target_pairs={{0,1},{1,0},{2,3},{3,2},{4,5},{5,4},{6,7},{7,6},{8,9},{9,8},{10,11... | collective-permute-start | bytes 49160 | tf_op jit(solution)/shard_map/ppermute | solution.py:331
  21.6 0.8 collective-permute-done.refs_0_
  22.4 0.0 collective-permute-done.2.refs_3_
  22.4 0.0 collective-permute-done.1.refs_2_
  22.4 2.5 %early_tiles.1 = (bf16[1024,512]{1,0:T(8,128)(2,1)S(1)}, bf16[1024,512]{1,0:T(8,128)(2,1)S(1)}) custom-call(bf16[16,512]{1,0:T(8,128)(2,1)S(1)} %collective-permute-done.refs_0_, bf16[16,512]{1,0:T(8,128)(2,1)S(1)} %get-tuple-element.20.refs_1_.refs_0_, bf16[144,256]{1,0:T(8,128)(2,1)S(1)} %collective-permute-done.1.refs_2_, ...), custom_call_target="tpu_custom_call" | custom-call | flops 268435456 | bytes 2097152 | tf_op jit(solution)/shard_map/early_tiles/pallas_call | solution.py:165
  25.0 0.0 collective-permute-done.5.refs_7_
  25.0 0.0 collective-permute-done.4.refs_6_
  25.0 2.0 %structure_factors.2 = (bf16[16,2,32,256]{3,2,1,0:T(8,128)(2,1)S(1)}, bf16[1024,512]{1,0:T(8,128)(2,1)S(1)}) custom-call(bf16[16,512]{1,0:T(8,128)(2,1)S(1)} %collective-permute-done.refs_0_, bf16[1024,512]{1,0:T(8,128)(2,1)S(1)} %get-tuple-element.22.refs_1_.refs_0_, bf16[144,256]{1,0:T(8,128)(2,1)S(1)} %collective-permute-done.1.refs_2_, ...), custom_call_target="tpu_custom_call" | custom-call | flops 536870912 | bytes 2097152 | tf_op jit(solution)/shard_map/structure_factors/pallas_call | solution.py:200
  27.0 3.4 %collective-permute-start.6 = (bf16[16,2,32,256]{3,2,1,0:T(8,128)(2,1)S(1)}, bf16[16,2,32,256]{3,2,1,0:T(8,128)(2,1)S(1)}, u32[]{:S(2)}, u32[]{:S(2)}) collective-permute-start(bf16[16,2,32,256]{3,2,1,0:T(8,128)(2,1)S(1)} %get-tuple-element.27), channel_id=1, source_target_pairs={{0,1},{1,0},{2,3},{3,2},{4,5},{5,4},{6,7},{7,6},{8,9},{9,8},{10,11... | collective-permute-start | bytes 1572872 | tf_op jit(solution)/shard_map/ppermute | solution.py:331
  30.4 0.0 copy-start.2
  30.4 2.0 %structure_factors.3 = (f32[16,2,32,256]{3,2,1,0:T(8,128)S(1)}, bf16[1024,512]{1,0:T(8,128)(2,1)S(1)}) custom-call(bf16[16,512]{1,0:T(8,128)(2,1)S(1)} %get-tuple-element.20.refs_1_.refs_0_, bf16[1024,512]{1,0:T(8,128)(2,1)S(1)} %get-tuple-element.24.refs_1_.refs_2_, bf16[144,256]{1,0:T(8,128)(2,1)S(1)} %collective-permute-done.1.refs_2_, ...), custom_call_target="tpu_custom_call" | custom-call | flops 536870912 | bytes 2097152 | tf_op jit(solution)/shard_map/structure_factors/pallas_call | solution.py:200
  32.4 0.0 collective-permute-done.6
  32.4 0.2 add_convert_fusion
  32.6 17.3 %all_to_all.10.refs_0_ = bf16[16,2,32,256]{3,2,1,0:T(8,128)(2,1)S(1)} all-to-all(bf16[16,2,32,256]{3,2,1,0:T(8,128)(2,1)S(1)} %add_convert_fusion), channel_id=1, replica_groups=mesh['z'=8,'y'=4,'x'=4,'core'=2] {'y','x'}, dimensions={0} | all-to-all | bytes 1048576 | tf_op jit(solution)/shard_map/all_to_all | solution.py:337
  49.9 0.0 copy-done.2
  49.9 0.4 filter_mix.1
  50.3 13.4 %all_to_all.11.refs_5_ = bf16[16,2,32,256]{3,2,1,0:T(8,128)(2,1)S(1)} all-to-all(bf16[16,2,32,256]{3,2,1,0:T(8,128)(2,1)S(1)} %filter_mix.1), channel_id=1, replica_groups=mesh['z'=8,'y'=4,'x'=4,'core'=2] {'y','x'}, dimensions={0} | all-to-all | bytes 1048576 | tf_op jit(solution)/shard_map/all_to_all | solution.py:337
  63.7 2.1 %collective-permute-start.7 = (bf16[16,2,32,256]{3,2,1,0:T(8,128)(2,1)S(1)}, bf16[16,2,32,256]{3,2,1,0:T(8,128)(2,1)S(1)}, u32[]{:S(2)}, u32[]{:S(2)}) collective-permute-start(bf16[16,2,32,256]{3,2,1,0:T(8,128)(2,1)S(1)} %all_to_all.11.refs_5_), channel_id=1, source_target_pairs={{0,1},{1,0},{2,3},{3,2},{4,5},{5,4},{6,7},{7,6},{8,9},{9,8},{10,11... | collective-permute-start | bytes 1572872 | tf_op jit(solution)/shard_map/ppermute | solution.py:331
  65.8 1.5 %collective-permute-done.7.refs_4_ = bf16[16,2,32,256]{3,2,1,0:T(8,128)(2,1)S(1)} collective-permute-done((bf16[16,2,32,256]{3,2,1,0:T(8,128)(2,1)S(1)}, bf16[16,2,32,256]{3,2,1,0:T(8,128)(2,1)S(1)}, u32[]{:S(2)}, u32[]{:S(2)}) %collective-permute-start.7) | collective-permute-done | bytes 524320 | tf_op jit(solution)/shard_map/ppermute | solution.py:331
  67.3 0.7 wave_fields.2
  68.1 2.6 %collective-permute-start.8 = (bf16[2,256,128]{2,1,0:T(8,128)(2,1)S(1)}, bf16[2,256,128]{2,1,0:T(8,128)(2,1)S(1)}, u32[]{:S(2)}, u32[]{:S(2)}) collective-permute-start(bf16[2,256,128]{2,1,0:T(8,128)(2,1)S(1)} %get-tuple-element.31), channel_id=1, source_target_pairs={{0,192},{32,224},{64,0},{96,32},{128,64},{160,96},{192,128},{224,1... | collective-permute-start | bytes 393224 | tf_op jit(solution)/shard_map/ppermute | solution.py:334
  70.7 0.0 copy-start
  70.7 0.0 copy-start.1
  70.7 0.0 copy-start.3
  70.7 0.0 copy-start.4
  70.7 0.6 collective-permute-start.9
  71.2 0.7 wave_fields.3
  72.0 3.3 %collective-permute-start.10 = (bf16[1,256,128]{2,1,0:T(8,128)(2,1)S(1)}, bf16[1,256,128]{2,1,0:T(8,128)(2,1)S(1)}, u32[]{:S(2)}, u32[]{:S(2)}) collective-permute-start(bf16[1,256,128]{2,1,0:T(8,128)(2,1)S(1)} %get-tuple-element.32), channel_id=1, source_target_pairs={{0,128},{32,160},{64,192},{96,224},{128,0},{160,32},{192,64},{224,... | collective-permute-start | bytes 196616 | tf_op jit(solution)/shard_map/ppermute | solution.py:334
  75.3 1.2 %collective-permute-done.8.refs_2_ = bf16[2,256,128]{2,1,0:T(8,128)(2,1)S(1)} collective-permute-done((bf16[2,256,128]{2,1,0:T(8,128)(2,1)S(1)}, bf16[2,256,128]{2,1,0:T(8,128)(2,1)S(1)}, u32[]{:S(2)}, u32[]{:S(2)}) %collective-permute-start.8) | collective-permute-done | bytes 131104 | tf_op jit(solution)/shard_map/ppermute | solution.py:334
  76.5 3.9 %collective-permute-start.12 = (bf16[1,256,128]{2,1,0:T(8,128)(2,1)S(1)}, bf16[1,256,128]{2,1,0:T(8,128)(2,1)S(1)}, u32[]{:S(2)}, u32[]{:S(2)}) collective-permute-start(bf16[1,256,128]{2,1,0:T(8,128)(2,1)S(1)} %add_convert_fusion.1), channel_id=1, source_target_pairs={{0,224},{32,0},{64,32},{96,64},{128,96},{160,128},{192,160},{224,1... | collective-permute-start | bytes 196616 | tf_op jit(solution)/shard_map/ppermute | solution.py:334
  80.4 0.0 collective-permute-done.9.refs_3_
  80.4 2.7 %collective-permute-start.11 = (bf16[1,256,128]{2,1,0:T(8,128)(2,1)S(1)}, bf16[1,256,128]{2,1,0:T(8,128)(2,1)S(1)}, u32[]{:S(2)}, u32[]{:S(2)}) collective-permute-start(bf16[1,256,128]{2,1,0:T(8,128)(2,1)S(1)} %add_convert_fusion.2), channel_id=1, source_target_pairs={{0,32},{32,64},{64,96},{96,128},{128,160},{160,192},{192,224},{224... | collective-permute-start | bytes 196616 | tf_op jit(solution)/shard_map/ppermute | solution.py:334
  83.2 0.0 collective-permute-done.10.refs_4_
  83.2 0.0 collective-permute-done.12.refs_6_
  83.2 1.7 %collective-permute-done.11.refs_5_ = bf16[1,256,128]{2,1,0:T(8,128)(2,1)S(1)} collective-permute-done((bf16[1,256,128]{2,1,0:T(8,128)(2,1)S(1)}, bf16[1,256,128]{2,1,0:T(8,128)(2,1)S(1)}, u32[]{:S(2)}, u32[]{:S(2)}) %collective-permute-start.11) | collective-permute-done | bytes 65568 | tf_op jit(solution)/shard_map/ppermute | solution.py:334
  84.8 0.0 copy-done
  84.8 0.0 copy-done.1
  84.8 0.0 copy-done.3
  84.8 0.0 copy-done.4
  84.9 1.2 %update_atoms.1 = bf16[128,256]{1,0:T(8,128)(2,1)} custom-call(s32[1]{0:T(128)S(6)} %copy.11.count_ref.refs_0_, f32[1,256,128]{2,1,0:T(8,128)S(1)} %get-tuple-element.30.refs_1_, bf16[2,256,128]{2,1,0:T(8,128)(2,1)S(1)} %collective-permute-done.8.refs_2_, bf16[2,256,128]{2,1,0:T(8,128)(2,1)S(1)} %collective-permute-done.9.refs_3_, ...), custom_call_target="tpu_custom_call" | custom-call | tf_op jit(solution)/shard_map/update_atoms/pallas_call | solution.py:310
  (4 shorter events, 0.0 us)
Async XLA Ops:
  1.5 9.7 %collective-permute-start.3 = (bf16[144,256]{1,0:T(8,128)(2,1)S(1)}, bf16[144,256]{1,0:T(8,128)(2,1)S(1)}, u32[]{:S(2)}, u32[]{:S(2)}) collective-permute-start(bf16[144,256]{1,0:T(8,128)(2,1)S(1)} %get-tuple-element.21.refs_5_), channel_id=1, source_target_pairs={{0,128},{32,160},{64,192},{96,224},{128,0},{160,32},{192,64},{224,... | collective-permute-start | bytes 221192 | tf_op jit(solution)/shard_map/ppermute | solution.py:334
  11.2 13.8 %collective-permute-start.5 = (bf16[288,256]{1,0:T(8,128)(2,1)S(1)}, bf16[288,256]{1,0:T(8,128)(2,1)S(1)}, u32[]{:S(2)}, u32[]{:S(2)}) collective-permute-start(bf16[288,256]{1,0:T(8,128)(2,1)S(1)} %constant_dynamic-update-slice_fusion), channel_id=1, source_target_pairs={{0,224},{32,0},{64,32},{96,64},{128,96},{160,128},{192,160},{224,1... | collective-permute-start | bytes 442376 | tf_op jit(solution)/shard_map/ppermute | solution.py:334
  16.0 9.0 %collective-permute-start.4 = (bf16[288,256]{1,0:T(8,128)(2,1)S(1)}, bf16[288,256]{1,0:T(8,128)(2,1)S(1)}, u32[]{:S(2)}, u32[]{:S(2)}) collective-permute-start(bf16[288,256]{1,0:T(8,128)(2,1)S(1)} %constant_dynamic-update-slice_fusion), channel_id=1, source_target_pairs={{0,32},{32,64},{64,96},{96,128},{128,160},{160,192},{192,224},{224... | collective-permute-start | bytes 442376 | tf_op jit(solution)/shard_map/ppermute | solution.py:334
  16.0 6.4 %collective-permute-start.2 = (bf16[144,256]{1,0:T(8,128)(2,1)S(1)}, bf16[144,256]{1,0:T(8,128)(2,1)S(1)}, u32[]{:S(2)}, u32[]{:S(2)}) collective-permute-start(bf16[144,256]{1,0:T(8,128)(2,1)S(1)} %get-tuple-element.21.refs_5_), channel_id=1, source_target_pairs={{0,64},{32,96},{64,128},{96,160},{128,192},{160,224},{192,0},{224,... | collective-permute-start | bytes 221192 | tf_op jit(solution)/shard_map/ppermute | solution.py:334
  16.0 6.4 %collective-permute-start.1 = (bf16[144,256]{1,0:T(8,128)(2,1)S(1)}, bf16[144,256]{1,0:T(8,128)(2,1)S(1)}, u32[]{:S(2)}, u32[]{:S(2)}) collective-permute-start(bf16[144,256]{1,0:T(8,128)(2,1)S(1)} %get-tuple-element.21.refs_5_), channel_id=1, source_target_pairs={{0,192},{32,224},{64,0},{96,32},{128,64},{160,96},{192,128},{224,1... | collective-permute-start | bytes 221192 | tf_op jit(solution)/shard_map/ppermute | solution.py:334
  19.6 2.9 %collective-permute-start = (bf16[16,512]{1,0:T(8,128)(2,1)S(1)}, bf16[16,512]{1,0:T(8,128)(2,1)S(1)}, u32[]{:S(2)}, u32[]{:S(2)}) collective-permute-start(bf16[16,512]{1,0:T(8,128)(2,1)S(1)} %get-tuple-element.20.refs_1_.refs_0_), channel_id=1, source_target_pairs={{0,1},{1,0},{2,3},{3,2},{4,5},{5,4},{6,7},{7,6},{8,9},{9,8},{10,11... | collective-permute-start | bytes 49160 | tf_op jit(solution)/shard_map/ppermute | solution.py:331
  27.0 5.4 %collective-permute-start.6 = (bf16[16,2,32,256]{3,2,1,0:T(8,128)(2,1)S(1)}, bf16[16,2,32,256]{3,2,1,0:T(8,128)(2,1)S(1)}, u32[]{:S(2)}, u32[]{:S(2)}) collective-permute-start(bf16[16,2,32,256]{3,2,1,0:T(8,128)(2,1)S(1)} %get-tuple-element.27), channel_id=1, source_target_pairs={{0,1},{1,0},{2,3},{3,2},{4,5},{5,4},{6,7},{7,6},{8,9},{9,8},{10,11... | collective-permute-start | bytes 1572872 | tf_op jit(solution)/shard_map/ppermute | solution.py:331
  30.4 19.5 %copy-start.2 = (f32[256,256]{1,0:T(8,128)S(1)}, f32[256,256]{1,0:T(8,128)}, u32[]{:S(2)}) copy-start(f32[256,256]{1,0:T(8,128)} %refs_2_.1) | copy-start | bytes 786436
  63.7 3.6 %collective-permute-start.7 = (bf16[16,2,32,256]{3,2,1,0:T(8,128)(2,1)S(1)}, bf16[16,2,32,256]{3,2,1,0:T(8,128)(2,1)S(1)}, u32[]{:S(2)}, u32[]{:S(2)}) collective-permute-start(bf16[16,2,32,256]{3,2,1,0:T(8,128)(2,1)S(1)} %all_to_all.11.refs_5_), channel_id=1, source_target_pairs={{0,1},{1,0},{2,3},{3,2},{4,5},{5,4},{6,7},{7,6},{8,9},{9,8},{10,11... | collective-permute-start | bytes 1572872 | tf_op jit(solution)/shard_map/ppermute | solution.py:331
  68.1 8.4 %collective-permute-start.8 = (bf16[2,256,128]{2,1,0:T(8,128)(2,1)S(1)}, bf16[2,256,128]{2,1,0:T(8,128)(2,1)S(1)}, u32[]{:S(2)}, u32[]{:S(2)}) collective-permute-start(bf16[2,256,128]{2,1,0:T(8,128)(2,1)S(1)} %get-tuple-element.31), channel_id=1, source_target_pairs={{0,192},{32,224},{64,0},{96,32},{128,64},{160,96},{192,128},{224,1... | collective-permute-start | bytes 393224 | tf_op jit(solution)/shard_map/ppermute | solution.py:334
  70.7 14.2 %copy-start = (bf16[256,1024]{1,0:T(8,128)(2,1)S(1)}, bf16[256,1024]{1,0:T(8,128)(2,1)}, u32[]{:S(2)}) copy-start(bf16[256,1024]{1,0:T(8,128)(2,1)} %refs_9_.1) | copy-start | bytes 1572868
  70.7 14.2 %copy-start.1 = (bf16[1024,256]{1,0:T(8,128)(2,1)S(1)}, bf16[1024,256]{1,0:T(8,128)(2,1)}, u32[]{:S(2)}) copy-start(bf16[1024,256]{1,0:T(8,128)(2,1)} %refs_10_.1) | copy-start | bytes 1572868
  70.7 14.2 %copy-start.3 = (bf16[128,256]{1,0:T(8,128)(2,1)S(1)}, bf16[128,256]{1,0:T(8,128)(2,1)}, u32[]{:S(2)}) copy-start(bf16[128,256]{1,0:T(8,128)(2,1)} %refs_7_.1) | copy-start | bytes 196612
  70.7 14.2 %copy-start.4 = (f32[256]{0:T(256)S(1)}, f32[256]{0:T(256)}, u32[]{:S(2)}) copy-start(f32[256]{0:T(256)} %param.15) | copy-start | bytes 3076
  70.7 9.8 %collective-permute-start.9 = (bf16[2,256,128]{2,1,0:T(8,128)(2,1)S(1)}, bf16[2,256,128]{2,1,0:T(8,128)(2,1)S(1)}, u32[]{:S(2)}, u32[]{:S(2)}) collective-permute-start(bf16[2,256,128]{2,1,0:T(8,128)(2,1)S(1)} %get-tuple-element.29.refs_6_), channel_id=1, source_target_pairs={{0,64},{32,96},{64,128},{96,160},{128,192},{160,224},{192,0},{224,... | collective-permute-start | bytes 393224 | tf_op jit(solution)/shard_map/ppermute | solution.py:334
  72.0 11.2 %collective-permute-start.10 = (bf16[1,256,128]{2,1,0:T(8,128)(2,1)S(1)}, bf16[1,256,128]{2,1,0:T(8,128)(2,1)S(1)}, u32[]{:S(2)}, u32[]{:S(2)}) collective-permute-start(bf16[1,256,128]{2,1,0:T(8,128)(2,1)S(1)} %get-tuple-element.32), channel_id=1, source_target_pairs={{0,128},{32,160},{64,192},{96,224},{128,0},{160,32},{192,64},{224,... | collective-permute-start | bytes 196616 | tf_op jit(solution)/shard_map/ppermute | solution.py:334
  76.5 6.7 %collective-permute-start.12 = (bf16[1,256,128]{2,1,0:T(8,128)(2,1)S(1)}, bf16[1,256,128]{2,1,0:T(8,128)(2,1)S(1)}, u32[]{:S(2)}, u32[]{:S(2)}) collective-permute-start(bf16[1,256,128]{2,1,0:T(8,128)(2,1)S(1)} %add_convert_fusion.1), channel_id=1, source_target_pairs={{0,224},{32,0},{64,32},{96,64},{128,96},{160,128},{192,160},{224,1... | collective-permute-start | bytes 196616 | tf_op jit(solution)/shard_map/ppermute | solution.py:334
  80.4 4.4 %collective-permute-start.11 = (bf16[1,256,128]{2,1,0:T(8,128)(2,1)S(1)}, bf16[1,256,128]{2,1,0:T(8,128)(2,1)S(1)}, u32[]{:S(2)}, u32[]{:S(2)}) collective-permute-start(bf16[1,256,128]{2,1,0:T(8,128)(2,1)S(1)} %add_convert_fusion.2), channel_id=1, source_target_pairs={{0,32},{32,64},{64,96},{96,128},{128,160},{160,192},{192,224},{224... | collective-permute-start | bytes 196616 | tf_op jit(solution)/shard_map/ppermute | solution.py:334
where the time goes:
time: 86.6 us; the launch traced here: 86.1 us
  starting transfers between devices  36.9 us (43%)
  blocking collectives  30.7 us (35%)
  Pallas kernels  10.4 us (12%)
  waiting for transfers between devices  7.05 us (8%)
    all_to_all x2, blocking collectives, exchange(): return lax.all_to_all(v, ('y', 'x'), 0, 0, tiled=True)  30.7 us
    ppermute x10, starting transfers between devices, shift(): lax.ppermute(v, 'z', [(i, (i + d) % NZ) for i in range(NZ)])  29.3 us
    ppermute x3, starting transfers between devices, partner(): return lax.ppermute(v, 'core', swap)  7.54 us
    ppermute x10, waiting for transfers between devices, shift(): lax.ppermute(v, 'z', [(i, (i + d) % NZ) for i in range(NZ)])  4.67 us
    pallas_call x2, Pallas kernels, factors(): pl.pallas_call(kernel, out_shape=(pltpu.VMEM((groups, 2, OWN, width), dty...  3.94 us
    pallas_call x1, Pallas kernels, early_tiles(): pl.pallas_call(kernel, out_shape=(pltpu.VMEM((2 * rows, atoms), bf16),) *...  2.54 us
    ppermute x3, waiting for transfers between devices, partner(): return lax.ppermute(v, 'core', swap)  2.38 us
  transfers between devices with their start and end apart: 13, of which 5 were waited for; matrix products, arithmetic and copies ran while one was open for 0% of the time, Pallas kernels for 6%

commit v1 on v0

--- a/solution.py
+++ b/solution.py
@@ -126,8 +126,7 @@
     for j, (source, k) in enumerate(layout):
         block = block_refs[source]
         at = k * (n + EXTRA)
-        if feats is not None:
-            feats[j * n : (j + 1) * n, :] = block[at : at + n, :]
+        feats[j * n : (j + 1) * n, :] = block[at : at + n, :]
         coords[:, j * n : (j + 1) * n] = block[at + n : at + n + EXTRA, 0:n]
 
 
@@ -150,51 +149,56 @@
     lax.fori_loop(0, rows // OWN, step, 0, unroll=2)
 
 
-def early_tiles(both_waves, blocks, layout):
+def early_factors(both_waves, blocks, layout):
     rows = both_waves[0].shape[1]
+    width = blocks[0].shape[1]
     n = blocks[0].shape[0] - EXTRA
     atoms = n * len(layout)
     nb = len(blocks)
 
     def kernel(*refs):
-        out_a, out_b, coords, turns = refs[2 + nb :]
-        load_blocks(refs[2 : 2 + nb], layout, None, coords)
-        fill_tile(refs[0], coords, turns, out_a)
-        fill_tile(refs[1], coords, turns, out_b)
-
+        tile_refs, sum_refs = refs[2 + nb : 4 + nb], refs[4 + nb : 6 + nb]
+        feats, coords, turns = refs[6 + nb :]
+        load_blocks(refs[2 : 2 + nb], layout, feats, coords)
+        for waves_ref, tile_ref, sum_ref in zip(refs[:2], tile_refs, sum_refs):
+            fill_tile(waves_ref, coords, turns, tile_ref)
+            sum_ref[...] = jnp.dot(tile_ref[...], feats[...], preferred_element_type=f32)
+
+    tile = pltpu.VMEM((2 * rows, atoms), bf16)
+    part = pltpu.VMEM((2 * rows, width), f32)
     return pl.pallas_call(
         kernel,
-        out_shape=(pltpu.VMEM((2 * rows, atoms), bf16),) * 2,
+        out_shape=(tile, tile, part, part),
         in_specs=[VMEM] * (2 + nb),
-        out_specs=(VMEM, VMEM),
-        scratch_shapes=[pltpu.VMEM((EXTRA, atoms), bf16), pltpu.VMEM((rows, atoms), f32)],
+        out_specs=(VMEM,) * 4,
+        scratch_shapes=[
+            pltpu.VMEM((atoms, width), bf16),
+            pltpu.VMEM((EXTRA, atoms), bf16),
+            pltpu.VMEM((rows, atoms), f32),
+        ],
         compiler_params=SMALL,
         cost_estimate=pl.CostEstimate(
-            flops=1024 * rows * atoms, transcendentals=0, bytes_accessed=8 * rows * atoms
-        ),
-        name="early_tiles",
+            flops=8 * rows * atoms * width, transcendentals=0, bytes_accessed=8 * rows * atoms
+        ),
+        name="early_factors",
     )(*on_chip(*both_waves, *blocks))
 
 
-def factors(waves9, tile, early, early_layout, late, late_layout, dtype):
+def factors(waves9, part, late, layout, dtype):
     rows = waves9.shape[1]
-    width = early[0].shape[1]
-    n = early[0].shape[0] - EXTRA
-    atoms = n * len(late_layout)
-    ready = n * len(early_layout)
+    width = late[0].shape[1]
+    n = sum(b.shape[0] for b in late) // len(layout) - EXTRA
+    atoms = n * len(layout)
     groups = rows // OWN
-    ne, nl = len(early), len(late)
+    nl = len(late)
 
     def kernel(*refs):
-        waves_ref, ready_ref = refs[:2]
-        early_refs = refs[2 : 2 + ne]
-        late_refs = refs[2 + ne : 2 + ne + nl]
-        out_ref, tile_ref, feats_a, feats_b, coords_a, coords_b, turns = refs[2 + ne + nl :]
-        load_blocks(early_refs, early_layout, feats_a, coords_a)
-        load_blocks(late_refs, late_layout, feats_b, coords_b)
-        fill_tile(waves_ref, coords_b, turns, tile_ref)
-        summed = jnp.dot(ready_ref[...], feats_a[...], preferred_element_type=f32)
-        summed = summed + jnp.dot(tile_ref[...], feats_b[...], preferred_element_type=f32)
+        waves_ref, part_ref = refs[:2]
+        out_ref, tile_ref, feats, coords, turns = refs[2 + nl :]
+        load_blocks(refs[2 : 2 + nl], layout, feats, coords)
+        fill_tile(waves_ref, coords, turns, tile_ref)
+        summed = jnp.dot(tile_ref[...], feats[...], preferred_element_type=f32)
+        summed = summed + part_ref[...]
         out_ref[...] = summed.astype(dtype).reshape(groups, 2, OWN, width)
 
     return pl.pallas_call(
@@ -203,21 +207,19 @@
             pltpu.VMEM((groups, 2, OWN, width), dtype),
             pltpu.VMEM((2 * rows, atoms), bf16),
         ),
-        in_specs=[VMEM] * (2 + ne + nl),
+        in_specs=[VMEM] * (2 + nl),
         out_specs=(VMEM, VMEM),
         scratch_shapes=[
-            pltpu.VMEM((ready, width), bf16),
             pltpu.VMEM((atoms, width), bf16),
-            pltpu.VMEM((EXTRA, ready), bf16),
             pltpu.VMEM((EXTRA, atoms), bf16),
             pltpu.VMEM((rows, atoms), f32),
         ],
         compiler_params=SMALL,
         cost_estimate=pl.CostEstimate(
-            flops=8 * rows * atoms * width, transcendentals=0, bytes_accessed=8 * rows * atoms
+            flops=4 * rows * atoms * width, transcendentals=0, bytes_accessed=8 * rows * atoms
         ),
         name="structure_factors",
-    )(*on_chip(waves9, tile, *early, *late))
+    )(*on_chip(waves9, part, *late))
 
 
 def filter_kernel(arrived_ref, filt_ref, mix_ref, out_ref, *, scale):
@@ -247,47 +249,59 @@
     )(*on_chip(arrived, filt, mixing))
 
 
-def fields(tiles, halves, outs, after=()):
-    owners, two, own, width = halves[0].shape
+def own_fields(tiles, half_of):
+    owners, two, own, width = half_of.shape
+    half = owners * two * own
+
+    def kernel(early_ref, late_ref, f_ref, early_out, late_out):
+        left = f_ref[...].reshape(half, width).T
+        early_out[...] = jnp.dot(left, early_ref[...], preferred_element_type=f32)
+        late_out[...] = jnp.dot(left, late_ref[...], preferred_element_type=f32)
+
+    return pl.pallas_call(
+        kernel,
+        out_shape=tuple(pltpu.VMEM((width, t.shape[1]), f32) for t in tiles),
+        in_specs=[VMEM] * 3,
+        out_specs=(VMEM,) * 2,
+        compiler_params=SMALL,
+        cost_estimate=pl.CostEstimate(
+            flops=4 * half * width * tiles[0].shape[1],
+            transcendentals=0,
+            bytes_accessed=4 * half * tiles[0].shape[1],
+        ),
+        name="own_fields",
+    )(*on_chip(*tiles, half_of))
+
+
+def fields(tiles, half_of, ready, outs):
+    owners, two, own, width = half_of.shape
     half = owners * two * own
     n = 128
-    wanted = [place for places, _ in outs for place in places]
-    first = min(j for _, j in wanted)
-    last = max(j for _, j in wanted) + 1
 
     def kernel(*refs):
-        tile_refs, half_refs = refs[:4], refs[4:6]
-        out_refs = refs[6 + len(after) :]
-        left = [f[...].reshape(half, width).T for f in half_refs]
-        got = []
-        for t in range(2):
-            field = None
-            for h in range(2):
-                part = jnp.dot(
-                    left[h],
-                    tile_refs[2 * h + t][:, first * n : last * n],
-                    preferred_element_type=f32,
-                )
-                field = part if field is None else field + part
-            got.append(field)
-        for out, (places, dtype) in zip(out_refs, outs):
+        tile_refs, f_ref, ready_refs = refs[:2], refs[2], refs[3:5]
+        left = f_ref[...].reshape(half, width).T
+        got = [
+            jnp.dot(left, tile[...], preferred_element_type=f32) + before[...]
+            for tile, before in zip(tile_refs, ready_refs)
+        ]
+        for out, (places, dtype) in zip(refs[5:], outs):
             for k, (t, j) in enumerate(places):
-                at = (j - first) * n
-                out[k] = got[t][:, at : at + n].astype(dtype)
+                out[k] = got[t][:, j * n : (j + 1) * n].astype(dtype)
 
     return pl.pallas_call(
         kernel,
         out_shape=tuple(pltpu.VMEM((len(places), width, n), d) for places, d in outs),
-        in_specs=[VMEM] * 6 + [pl.BlockSpec(memory_space=pl.ANY)] * len(after),
+        in_specs=[VMEM] * 5,
         out_specs=(VMEM,) * len(outs),
         compiler_params=SMALL,
         cost_estimate=pl.CostEstimate(
-            flops=4 * half * width * n * len(wanted),
+            flops=4 * half * width * tiles[0].shape[1],
             transcendentals=0,
-            bytes_accessed=4 * half * n * len(wanted),
+            bytes_accessed=4 * half * tiles[0].shape[1],
         ),
         name="wave_fields",
-    )(*on_chip(*tiles, *halves), *after)
+    )(*on_chip(*tiles, half_of, *ready))
 
 
 def update_kernel(count_ref, *refs, scale):
@@ -350,24 +364,29 @@
     early_layout = [(0, 0), (1, 0), (2, 0), (3, 0)]
     late = [near_behind, near_ahead]
     late_layout = [(0, 1), (1, 1), (1, 0), (0, 0)]
-    ready_other, ready_mine = early_tiles([other, mine], early, early_layout)
-    sent, tile_other = factors(other, ready_other, early, early_layout, late, late_layout, bf16)
+    ready_other, ready_mine, part_other, part_mine = early_factors(
+        [other, mine], early, early_layout
+    )
+    sent, tile_other = factors(other, part_other, late, late_layout, bf16)
     arrived = partner(sent)
-    kept, tile_mine = factors(mine, ready_mine, early, early_layout, late, late_layout, f32)
+    kept, tile_mine = factors(mine, part_mine, late, late_layout, f32)
     summed = exchange((kept + arrived.astype(f32)).astype(bf16))
     spread = filter_mix(summed, filt, mixing, 1.0 / math.sqrt(atoms_all))
     filtered = exchange(spread)
-    halves = (partner(filtered), filtered)
-
-    tiles = (ready_other, tile_other, ready_mine, tile_mine)
-    to_ahead, to_behind = fields(
-        tiles, halves, [([(0, 0), (1, 0)], bf16), ([(0, 1), (1, 1)], bf16)]
-    )
-    far, own, one_ahead, one_behind = fields(
-        tiles,
-        halves,
-        [([(0, 2)], bf16), ([(0, 3)], f32), ([(1, 2)], f32), ([(1, 3)], f32)],
-        (to_ahead,),
+    filtered_other = partner(filtered)
+    ready = own_fields((ready_mine, tile_mine), filtered)
+    to_ahead, to_behind, far, own, one_ahead, one_behind = fields(
+        (ready_other, tile_other),
+        filtered_other,
+        ready,
+        [
+            ([(0, 0), (1, 0)], bf16),
+            ([(0, 1), (1, 1)], bf16),
+            ([(0, 2)], bf16),
+            ([(0, 3)], f32),
+            ([(1, 2)], f32),
+            ([(1, 3)], f32),
+        ],
     )
     from_behind = shift(to_ahead, 2)
     from_ahead = shift(to_behind, -2)

time: 86.6 us -> 90.5 us (1.045)
  waiting for transfers between devices: 7.05 us -> 9.45 us
    ppermute x10, waiting for transfers between devices: 4.67 us -> 7.81 us  [shift(): lax.ppermute(v, 'z', [(i, (i + d) % NZ) for i in range(NZ)])]
    pallas_call x1 -> x2, Pallas kernels: 2.54 us -> 4.4 us  [the longest x1 3.68 us: early_factors(): pl.pallas_call(kernel, out_shape=(tile, tile, part, part), in_specs=[VMEM...]
  transfers between devices with their start and end apart: 13 -> 13, of which waited for: 5 -> 6; matrix products, arithmetic and copies ran while one was open for 0% -> 0% of each run, Pallas kernels for 6% -> 7%
where the time goes in v1:
time: 90.5 us; the launch traced here: 89.7 us
  starting transfers between devices  37.7 us (42%)
  blocking collectives  30.6 us (34%)
  Pallas kernels  11 us (12%)
  waiting for transfers between devices  9.45 us (10%)
    all_to_all x2, blocking collectives, exchange(): return lax.all_to_all(v, ('y', 'x'), 0, 0, tiled=True)  30.6 us
    ppermute x10, starting transfers between devices, shift(): lax.ppermute(v, 'z', [(i, (i + d) % NZ) for i in range(NZ)])  30.1 us
    ppermute x10, waiting for transfers between devices, shift(): lax.ppermute(v, 'z', [(i, (i + d) % NZ) for i in range(NZ)])  7.81 us
    ppermute x3, starting transfers between devices, partner(): return lax.ppermute(v, 'core', swap)  7.6 us
    pallas_call x1, Pallas kernels, early_factors(): pl.pallas_call(kernel, out_shape=(tile, tile, part, part), in_specs=[VMEM...  3.68 us
    pallas_call x2, Pallas kernels, factors(): pl.pallas_call(kernel, out_shape=(pltpu.VMEM((groups, 2, OWN, width), dty...  3.39 us
  transfers between devices with their start and end apart: 13, of which 6 were waited for; matrix products, arithmetic and copies ran while one was open for 0% of the time, Pallas kernels for 7%

profile of v1, /device:TPU:1, one launch (start us, length us, event | category | flops | bytes accessed | tf_op | source)
XLA Modules:
  0.0 89.7 jit_solution(14635704476154011968)
XLA Ops:
  0.7 0.9 pack_atoms.1
  1.5 7.8 %collective-permute-start.3 = (bf16[144,256]{1,0:T(8,128)(2,1)S(1)}, bf16[144,256]{1,0:T(8,128)(2,1)S(1)}, u32[]{:S(2)}, u32[]{:S(2)}) collective-permute-start(bf16[144,256]{1,0:T(8,128)(2,1)S(1)} %get-tuple-element.25.refs_5_), channel_id=1, source_target_pairs={{0,128},{32,160},{64,192},{96,224},{128,0},{160,32},{192,64},{224,... | collective-permute-start | bytes 221192 | tf_op jit(solution)/shard_map/ppermute | solution.py:348
  9.3 1.8 %collective-permute-done.3.refs_4_ = bf16[144,256]{1,0:T(8,128)(2,1)S(1)} collective-permute-done((bf16[144,256]{1,0:T(8,128)(2,1)S(1)}, bf16[144,256]{1,0:T(8,128)(2,1)S(1)}, u32[]{:S(2)}, u32[]{:S(2)}) %collective-permute-start.3) | collective-permute-done | bytes 73760 | tf_op jit(solution)/shard_map/ppermute | solution.py:348
  11.2 4.8 %collective-permute-start.5 = (bf16[288,256]{1,0:T(8,128)(2,1)S(1)}, bf16[288,256]{1,0:T(8,128)(2,1)S(1)}, u32[]{:S(2)}, u32[]{:S(2)}) collective-permute-start(bf16[288,256]{1,0:T(8,128)(2,1)S(1)} %constant_dynamic-update-slice_fusion), channel_id=1, source_target_pairs={{0,224},{32,0},{64,32},{96,64},{128,96},{160,128},{192,160},{224,1... | collective-permute-start | bytes 442376 | tf_op jit(solution)/shard_map/ppermute | solution.py:348
  16.0 0.0 collective-permute-start.4
  16.0 0.0 collective-permute-start.2
  16.0 3.6 %collective-permute-start.1 = (bf16[144,256]{1,0:T(8,128)(2,1)S(1)}, bf16[144,256]{1,0:T(8,128)(2,1)S(1)}, u32[]{:S(2)}, u32[]{:S(2)}) collective-permute-start(bf16[144,256]{1,0:T(8,128)(2,1)S(1)} %get-tuple-element.25.refs_5_), channel_id=1, source_target_pairs={{0,192},{32,224},{64,0},{96,32},{128,64},{160,96},{192,128},{224,1... | collective-permute-start | bytes 221192 | tf_op jit(solution)/shard_map/ppermute | solution.py:348
  19.6 2.0 %collective-permute-start = (bf16[16,512]{1,0:T(8,128)(2,1)S(1)}, bf16[16,512]{1,0:T(8,128)(2,1)S(1)}, u32[]{:S(2)}, u32[]{:S(2)}) collective-permute-start(bf16[16,512]{1,0:T(8,128)(2,1)S(1)} %get-tuple-element.24.refs_1_.refs_0_), channel_id=1, source_target_pairs={{0,1},{1,0},{2,3},{3,2},{4,5},{5,4},{6,7},{7,6},{8,9},{9,8},{10,11... | collective-permute-start | bytes 49160 | tf_op jit(solution)/shard_map/ppermute | solution.py:345
  21.6 0.8 collective-permute-done.refs_0_
  22.4 0.0 collective-permute-done.2.refs_3_
  22.4 0.0 collective-permute-done.1.refs_2_
  22.4 3.7 %early_factors.1 = (bf16[1024,512]{1,0:T(8,128)(2,1)S(1)}, bf16[1024,512]{1,0:T(8,128)(2,1)S(1)}, f32[1024,256]{1,0:T(8,128)S(1)}, f32[1024,256]{1,0:T(8,128)S(1)}) custom-call(bf16[16,512]{1,0:T(8,128)(2,1)S(1)} %collective-permute-done.refs_0_, bf16[16,512]{1,0:T(8,128)(2,1)S(1)} %get-tuple-element.24.refs_1_.refs_0_, ...), custom_call_target="tpu_custom_call" | custom-call | flops 536870912 | bytes 2097152 | tf_op jit(solution)/shard_map/early_factors/pallas_call | solution.py:169
  26.1 0.0 collective-permute-done.5.refs_3_
  26.1 0.0 collective-permute-done.4.refs_2_
  26.1 1.7 %structure_factors.2 = (bf16[16,2,32,256]{3,2,1,0:T(8,128)(2,1)S(1)}, bf16[1024,512]{1,0:T(8,128)(2,1)S(1)}) custom-call(bf16[16,512]{1,0:T(8,128)(2,1)S(1)} %collective-permute-done.refs_0_, f32[1024,256]{1,0:T(8,128)S(1)} %get-tuple-element.27.refs_1_, bf16[288,256]{1,0:T(8,128)(2,1)S(1)} %collective-permute-done.4.refs_2_, ...), custom_call_target="tpu_custom_call" | custom-call | flops 268435456 | bytes 2097152 | tf_op jit(solution)/shard_map/structure_factors/pallas_call | solution.py:204
  27.8 3.4 %collective-permute-start.6 = (bf16[16,2,32,256]{3,2,1,0:T(8,128)(2,1)S(1)}, bf16[16,2,32,256]{3,2,1,0:T(8,128)(2,1)S(1)}, u32[]{:S(2)}, u32[]{:S(2)}) collective-permute-start(bf16[16,2,32,256]{3,2,1,0:T(8,128)(2,1)S(1)} %get-tuple-element.31), channel_id=1, source_target_pairs={{0,1},{1,0},{2,3},{3,2},{4,5},{5,4},{6,7},{7,6},{8,9},{9,8},{10,11... | collective-permute-start | bytes 1572872 | tf_op jit(solution)/shard_map/ppermute | solution.py:345
  31.3 0.0 copy-start.2
  31.3 1.7 %structure_factors.3 = (f32[16,2,32,256]{3,2,1,0:T(8,128)S(1)}, bf16[1024,512]{1,0:T(8,128)(2,1)S(1)}) custom-call(bf16[16,512]{1,0:T(8,128)(2,1)S(1)} %get-tuple-element.24.refs_1_.refs_0_, f32[1024,256]{1,0:T(8,128)S(1)} %get-tuple-element.29.refs_1_, bf16[288,256]{1,0:T(8,128)(2,1)S(1)} %collective-permute-done.4.refs_2_, ...), custom_call_target="tpu_custom_call" | custom-call | flops 268435456 | bytes 2097152 | tf_op jit(solution)/shard_map/structure_factors/pallas_call | solution.py:204
  33.0 0.0 collective-permute-done.6
  33.0 0.2 add_convert_fusion
  33.2 17.1 %all_to_all.10.refs_0_ = bf16[16,2,32,256]{3,2,1,0:T(8,128)(2,1)S(1)} all-to-all(bf16[16,2,32,256]{3,2,1,0:T(8,128)(2,1)S(1)} %add_convert_fusion), channel_id=1, replica_groups=mesh['z'=8,'y'=4,'x'=4,'core'=2] {'y','x'}, dimensions={0} | all-to-all | bytes 1048576 | tf_op jit(solution)/shard_map/all_to_all | solution.py:351
  50.3 0.0 copy-done.2
  50.3 0.4 filter_mix.1
  50.7 13.5 %all_to_all.11.f_ref = bf16[16,2,32,256]{3,2,1,0:T(8,128)(2,1)S(1)} all-to-all(bf16[16,2,32,256]{3,2,1,0:T(8,128)(2,1)S(1)} %filter_mix.1), channel_id=1, replica_groups=mesh['z'=8,'y'=4,'x'=4,'core'=2] {'y','x'}, dimensions={0} | all-to-all | bytes 1048576 | tf_op jit(solution)/shard_map/all_to_all | solution.py:351
  64.1 2.1 %collective-permute-start.7 = (bf16[16,2,32,256]{3,2,1,0:T(8,128)(2,1)S(1)}, bf16[16,2,32,256]{3,2,1,0:T(8,128)(2,1)S(1)}, u32[]{:S(2)}, u32[]{:S(2)}) collective-permute-start(bf16[16,2,32,256]{3,2,1,0:T(8,128)(2,1)S(1)} %all_to_all.11.f_ref), channel_id=1, source_target_pairs={{0,1},{1,0},{2,3},{3,2},{4,5},{5,4},{6,7},{7,6},{8,9},{9,8},{10,11... | collective-permute-start | bytes 1572872 | tf_op jit(solution)/shard_map/ppermute | solution.py:345
  66.3 0.7 own_fields.1
  67.0 0.8 collective-permute-done.7.refs_2_
  67.8 0.0 copy-start
  67.8 0.0 copy-start.1
  67.8 0.0 copy-start.3
  67.8 0.0 copy-start.4
  67.8 0.7 wave_fields.1
  68.6 2.5 %collective-permute-start.8 = (bf16[2,256,128]{2,1,0:T(8,128)(2,1)S(1)}, bf16[2,256,128]{2,1,0:T(8,128)(2,1)S(1)}, u32[]{:S(2)}, u32[]{:S(2)}) collective-permute-start(bf16[2,256,128]{2,1,0:T(8,128)(2,1)S(1)} %get-tuple-element.38), channel_id=1, source_target_pairs={{0,192},{32,224},{64,0},{96,32},{128,64},{160,96},{192,128},{224,1... | collective-permute-start | bytes 393224 | tf_op jit(solution)/shard_map/ppermute | solution.py:348
  71.1 3.7 %collective-permute-start.10 = (bf16[1,256,128]{2,1,0:T(8,128)(2,1)S(1)}, bf16[1,256,128]{2,1,0:T(8,128)(2,1)S(1)}, u32[]{:S(2)}, u32[]{:S(2)}) collective-permute-start(bf16[1,256,128]{2,1,0:T(8,128)(2,1)S(1)} %get-tuple-element.40), channel_id=1, source_target_pairs={{0,128},{32,160},{64,192},{96,224},{128,0},{160,32},{192,64},{224,... | collective-permute-start | bytes 196616 | tf_op jit(solution)/shard_map/ppermute | solution.py:348
  74.9 0.0 collective-permute-start.9
  74.9 2.1 %collective-permute-done.8.refs_2_ = bf16[2,256,128]{2,1,0:T(8,128)(2,1)S(1)} collective-permute-done((bf16[2,256,128]{2,1,0:T(8,128)(2,1)S(1)}, bf16[2,256,128]{2,1,0:T(8,128)(2,1)S(1)}, u32[]{:S(2)}, u32[]{:S(2)}) %collective-permute-start.8) | collective-permute-done | bytes 131104 | tf_op jit(solution)/shard_map/ppermute | solution.py:348
  76.9 4.0 %collective-permute-start.12 = (bf16[1,256,128]{2,1,0:T(8,128)(2,1)S(1)}, bf16[1,256,128]{2,1,0:T(8,128)(2,1)S(1)}, u32[]{:S(2)}, u32[]{:S(2)}) collective-permute-start(bf16[1,256,128]{2,1,0:T(8,128)(2,1)S(1)} %add_convert_fusion.1), channel_id=1, source_target_pairs={{0,224},{32,0},{64,32},{96,64},{128,96},{160,128},{192,160},{224,1... | collective-permute-start | bytes 196616 | tf_op jit(solution)/shard_map/ppermute | solution.py:348
  80.9 2.6 %collective-permute-done.9.refs_3_ = bf16[2,256,128]{2,1,0:T(8,128)(2,1)S(1)} collective-permute-done((bf16[2,256,128]{2,1,0:T(8,128)(2,1)S(1)}, bf16[2,256,128]{2,1,0:T(8,128)(2,1)S(1)}, u32[]{:S(2)}, u32[]{:S(2)}) %collective-permute-start.9) | collective-permute-done | bytes 131104 | tf_op jit(solution)/shard_map/ppermute | solution.py:348
  83.5 3.7 %collective-permute-start.11 = (bf16[1,256,128]{2,1,0:T(8,128)(2,1)S(1)}, bf16[1,256,128]{2,1,0:T(8,128)(2,1)S(1)}, u32[]{:S(2)}, u32[]{:S(2)}) collective-permute-start(bf16[1,256,128]{2,1,0:T(8,128)(2,1)S(1)} %add_convert_fusion.2), channel_id=1, source_target_pairs={{0,32},{32,64},{64,96},{96,128},{128,160},{160,192},{192,224},{224... | collective-permute-start | bytes 196616 | tf_op jit(solution)/shard_map/ppermute | solution.py:348
  87.2 0.0 collective-permute-done.10.refs_4_
  87.2 0.0 collective-permute-done.12.refs_6_
  87.2 1.3 %collective-permute-done.11.refs_5_ = bf16[1,256,128]{2,1,0:T(8,128)(2,1)S(1)} collective-permute-done((bf16[1,256,128]{2,1,0:T(8,128)(2,1)S(1)}, bf16[1,256,128]{2,1,0:T(8,128)(2,1)S(1)}, u32[]{:S(2)}, u32[]{:S(2)}) %collective-permute-start.11) | collective-permute-done | bytes 65568 | tf_op jit(solution)/shard_map/ppermute | solution.py:348
  88.5 0.0 copy-done
  88.5 0.0 copy-done.1
  88.5 0.0 copy-done.3
  88.5 0.0 copy-done.4
  88.5 1.2 %update_atoms.1 = bf16[128,256]{1,0:T(8,128)(2,1)} custom-call(s32[1]{0:T(128)S(6)} %copy.11.count_ref.refs_0_, f32[1,256,128]{2,1,0:T(8,128)S(1)} %get-tuple-element.37.refs_1_, bf16[2,256,128]{2,1,0:T(8,128)(2,1)S(1)} %collective-permute-done.8.refs_2_, bf16[2,256,128]{2,1,0:T(8,128)(2,1)S(1)} %collective-permute-done.9.refs_3_, ...), custom_call_target="tpu_custom_call" | custom-call | tf_op jit(solution)/shard_map/update_atoms/pallas_call | solution.py:324
  (4 shorter events, 0.0 us)
Async XLA Ops:
  1.5 9.7 %collective-permute-start.3 = (bf16[144,256]{1,0:T(8,128)(2,1)S(1)}, bf16[144,256]{1,0:T(8,128)(2,1)S(1)}, u32[]{:S(2)}, u32[]{:S(2)}) collective-permute-start(bf16[144,256]{1,0:T(8,128)(2,1)S(1)} %get-tuple-element.25.refs_5_), channel_id=1, source_target_pairs={{0,128},{32,160},{64,192},{96,224},{128,0},{160,32},{192,64},{224,... | collective-permute-start | bytes 221192 | tf_op jit(solution)/shard_map/ppermute | solution.py:348
  11.2 14.9 %collective-permute-start.5 = (bf16[288,256]{1,0:T(8,128)(2,1)S(1)}, bf16[288,256]{1,0:T(8,128)(2,1)S(1)}, u32[]{:S(2)}, u32[]{:S(2)}) collective-permute-start(bf16[288,256]{1,0:T(8,128)(2,1)S(1)} %constant_dynamic-update-slice_fusion), channel_id=1, source_target_pairs={{0,224},{32,0},{64,32},{96,64},{128,96},{160,128},{192,160},{224,1... | collective-permute-start | bytes 442376 | tf_op jit(solution)/shard_map/ppermute | solution.py:348
  16.0 10.1 %collective-permute-start.4 = (bf16[288,256]{1,0:T(8,128)(2,1)S(1)}, bf16[288,256]{1,0:T(8,128)(2,1)S(1)}, u32[]{:S(2)}, u32[]{:S(2)}) collective-permute-start(bf16[288,256]{1,0:T(8,128)(2,1)S(1)} %constant_dynamic-update-slice_fusion), channel_id=1, source_target_pairs={{0,32},{32,64},{64,96},{96,128},{128,160},{160,192},{192,224},{224... | collective-permute-start | bytes 442376 | tf_op jit(solution)/shard_map/ppermute | solution.py:348
  16.0 6.4 %collective-permute-start.2 = (bf16[144,256]{1,0:T(8,128)(2,1)S(1)}, bf16[144,256]{1,0:T(8,128)(2,1)S(1)}, u32[]{:S(2)}, u32[]{:S(2)}) collective-permute-start(bf16[144,256]{1,0:T(8,128)(2,1)S(1)} %get-tuple-element.25.refs_5_), channel_id=1, source_target_pairs={{0,64},{32,96},{64,128},{96,160},{128,192},{160,224},{192,0},{224,... | collective-permute-start | bytes 221192 | tf_op jit(solution)/shard_map/ppermute | solution.py:348
  16.0 6.4 %collective-permute-start.1 = (bf16[144,256]{1,0:T(8,128)(2,1)S(1)}, bf16[144,256]{1,0:T(8,128)(2,1)S(1)}, u32[]{:S(2)}, u32[]{:S(2)}) collective-permute-start(bf16[144,256]{1,0:T(8,128)(2,1)S(1)} %get-tuple-element.25.refs_5_), channel_id=1, source_target_pairs={{0,192},{32,224},{64,0},{96,32},{128,64},{160,96},{192,128},{224,1... | collective-permute-start | bytes 221192 | tf_op jit(solution)/shard_map/ppermute | solution.py:348
  19.6 2.9 %collective-permute-start = (bf16[16,512]{1,0:T(8,128)(2,1)S(1)}, bf16[16,512]{1,0:T(8,128)(2,1)S(1)}, u32[]{:S(2)}, u32[]{:S(2)}) collective-permute-start(bf16[16,512]{1,0:T(8,128)(2,1)S(1)} %get-tuple-element.24.refs_1_.refs_0_), channel_id=1, source_target_pairs={{0,1},{1,0},{2,3},{3,2},{4,5},{5,4},{6,7},{7,6},{8,9},{9,8},{10,11... | collective-permute-start | bytes 49160 | tf_op jit(solution)/shard_map/ppermute | solution.py:345
  27.8 5.1 %collective-permute-start.6 = (bf16[16,2,32,256]{3,2,1,0:T(8,128)(2,1)S(1)}, bf16[16,2,32,256]{3,2,1,0:T(8,128)(2,1)S(1)}, u32[]{:S(2)}, u32[]{:S(2)}) collective-permute-start(bf16[16,2,32,256]{3,2,1,0:T(8,128)(2,1)S(1)} %get-tuple-element.31), channel_id=1, source_target_pairs={{0,1},{1,0},{2,3},{3,2},{4,5},{5,4},{6,7},{7,6},{8,9},{9,8},{10,11... | collective-permute-start | bytes 1572872 | tf_op jit(solution)/shard_map/ppermute | solution.py:345
  31.3 19.0 %copy-start.2 = (f32[256,256]{1,0:T(8,128)S(1)}, f32[256,256]{1,0:T(8,128)}, u32[]{:S(2)}) copy-start(f32[256,256]{1,0:T(8,128)} %refs_2_.1) | copy-start | bytes 786436
  64.1 3.7 %collective-permute-start.7 = (bf16[16,2,32,256]{3,2,1,0:T(8,128)(2,1)S(1)}, bf16[16,2,32,256]{3,2,1,0:T(8,128)(2,1)S(1)}, u32[]{:S(2)}, u32[]{:S(2)}) collective-permute-start(bf16[16,2,32,256]{3,2,1,0:T(8,128)(2,1)S(1)} %all_to_all.11.f_ref), channel_id=1, source_target_pairs={{0,1},{1,0},{2,3},{3,2},{4,5},{5,4},{6,7},{7,6},{8,9},{9,8},{10,11... | collective-permute-start | bytes 1572872 | tf_op jit(solution)/shard_map/ppermute | solution.py:345
  67.8 20.7 %copy-start = (bf16[256,1024]{1,0:T(8,128)(2,1)S(1)}, bf16[256,1024]{1,0:T(8,128)(2,1)}, u32[]{:S(2)}) copy-start(bf16[256,1024]{1,0:T(8,128)(2,1)} %refs_9_.1) | copy-start | bytes 1572868
  67.8 20.7 %copy-start.1 = (bf16[1024,256]{1,0:T(8,128)(2,1)S(1)}, bf16[1024,256]{1,0:T(8,128)(2,1)}, u32[]{:S(2)}) copy-start(bf16[1024,256]{1,0:T(8,128)(2,1)} %refs_10_.1) | copy-start | bytes 1572868
  67.8 20.7 %copy-start.3 = (bf16[128,256]{1,0:T(8,128)(2,1)S(1)}, bf16[128,256]{1,0:T(8,128)(2,1)}, u32[]{:S(2)}) copy-start(bf16[128,256]{1,0:T(8,128)(2,1)} %refs_7_.1) | copy-start | bytes 196612
  67.8 20.7 %copy-start.4 = (f32[256]{0:T(256)S(1)}, f32[256]{0:T(256)}, u32[]{:S(2)}) copy-start(f32[256]{0:T(256)} %param.15) | copy-start | bytes 3076
  68.6 8.3 %collective-permute-start.8 = (bf16[2,256,128]{2,1,0:T(8,128)(2,1)S(1)}, bf16[2,256,128]{2,1,0:T(8,128)(2,1)S(1)}, u32[]{:S(2)}, u32[]{:S(2)}) collective-permute-start(bf16[2,256,128]{2,1,0:T(8,128)(2,1)S(1)} %get-tuple-element.38), channel_id=1, source_target_pairs={{0,192},{32,224},{64,0},{96,32},{128,64},{160,96},{192,128},{224,1... | collective-permute-start | bytes 393224 | tf_op jit(solution)/shard_map/ppermute | solution.py:348
  71.1 16.0 %collective-permute-start.10 = (bf16[1,256,128]{2,1,0:T(8,128)(2,1)S(1)}, bf16[1,256,128]{2,1,0:T(8,128)(2,1)S(1)}, u32[]{:S(2)}, u32[]{:S(2)}) collective-permute-start(bf16[1,256,128]{2,1,0:T(8,128)(2,1)S(1)} %get-tuple-element.40), channel_id=1, source_target_pairs={{0,128},{32,160},{64,192},{96,224},{128,0},{160,32},{192,64},{224,... | collective-permute-start | bytes 196616 | tf_op jit(solution)/shard_map/ppermute | solution.py:348
  74.9 8.6 %collective-permute-start.9 = (bf16[2,256,128]{2,1,0:T(8,128)(2,1)S(1)}, bf16[2,256,128]{2,1,0:T(8,128)(2,1)S(1)}, u32[]{:S(2)}, u32[]{:S(2)}) collective-permute-start(bf16[2,256,128]{2,1,0:T(8,128)(2,1)S(1)} %get-tuple-element.39), channel_id=1, source_target_pairs={{0,64},{32,96},{64,128},{96,160},{128,192},{160,224},{192,0},{224,... | collective-permute-start | bytes 393224 | tf_op jit(solution)/shard_map/ppermute | solution.py:348
  76.9 10.2 %collective-permute-start.12 = (bf16[1,256,128]{2,1,0:T(8,128)(2,1)S(1)}, bf16[1,256,128]{2,1,0:T(8,128)(2,1)S(1)}, u32[]{:S(2)}, u32[]{:S(2)}) collective-permute-start(bf16[1,256,128]{2,1,0:T(8,128)(2,1)S(1)} %add_convert_fusion.1), channel_id=1, source_target_pairs={{0,224},{32,0},{64,32},{96,64},{128,96},{160,128},{192,160},{224,1... | collective-permute-start | bytes 196616 | tf_op jit(solution)/shard_map/ppermute | solution.py:348
  83.5 5.0 %collective-permute-start.11 = (bf16[1,256,128]{2,1,0:T(8,128)(2,1)S(1)}, bf16[1,256,128]{2,1,0:T(8,128)(2,1)S(1)}, u32[]{:S(2)}, u32[]{:S(2)}) collective-permute-start(bf16[1,256,128]{2,1,0:T(8,128)(2,1)S(1)} %add_convert_fusion.2), channel_id=1, source_target_pairs={{0,32},{32,64},{64,96},{96,128},{128,160},{160,192},{192,224},{224... | collective-permute-start | bytes 196616 | tf_op jit(solution)/shard_map/ppermute | solution.py:348

commit v2 on v1

--- a/solution.py
+++ b/solution.py
@@ -146,7 +146,7 @@
             tile_ref[to_sin, :] = s.astype(bf16)
         return carry
 
-    lax.fori_loop(0, rows // OWN, step, 0, unroll=2)
+    lax.fori_loop(0, rows // OWN, step, 0, unroll=4)
 
 
 def early_factors(both_waves, blocks, layout):
@@ -304,13 +304,28 @@
     )(*on_chip(*tiles, half_of, *ready))
 
 
-def update_kernel(count_ref, *refs, scale):
-    part_refs = refs[:-5]
-    feats_ref, gain_ref, win_ref, wout_ref, out_ref = refs[-5:]
+def early_state_kernel(*refs, scale):
+    part_refs, feats_ref, out_ref = refs[:-2], refs[-2], refs[-1]
     total = part_refs[0][0].astype(f32)
     for part in part_refs[1:]:
         total = total + part[0].astype(f32)
-    state = feats_ref[...].astype(f32) + (total * scale).T
+    out_ref[...] = feats_ref[...].astype(f32) + (total * scale).T
+
+
+def early_state(parts, feats, scale):
+    return pl.pallas_call(
+        lambda *refs: early_state_kernel(*refs, scale=scale),
+        out_shape=pltpu.VMEM(feats.shape, f32),
+        in_specs=[VMEM] * (len(parts) + 1),
+        out_specs=VMEM,
+        compiler_params=SMALL,
+        name="early_state",
+    )(*on_chip(*parts, feats))
+
+
+def update_kernel(count_ref, near_a, near_b, state_ref, gain_ref, win_ref, wout_ref, out_ref, *, scale):
+    near = near_a[0].astype(f32) + near_b[0].astype(f32)
+    state = state_ref[...] + (near * scale).T
     meansq = jnp.mean(state * state, axis=1, keepdims=True)
     normed = (state * lax.rsqrt(meansq + 1e-06) * gain_ref[...]).astype(bf16)
     v = jnp.dot(normed, win_ref[...], preferred_element_type=f32)
@@ -320,15 +335,15 @@
     out_ref[...] = jnp.where(slot < count_ref[0], result, 0.0).astype(bf16)
 
 
-def update(counts, parts, feats, gain, w_in, w_out, scale):
+def update(counts, near, state, gain, w_in, w_out, scale):
     return pl.pallas_call(
         lambda *refs: update_kernel(*refs, scale=scale),
-        out_shape=jax.ShapeDtypeStruct(feats.shape, bf16),
-        in_specs=[pl.BlockSpec(memory_space=pltpu.SMEM)] + [VMEM] * (len(parts) + 4),
+        out_shape=jax.ShapeDtypeStruct(state.shape, bf16),
+        in_specs=[pl.BlockSpec(memory_space=pltpu.SMEM)] + [VMEM] * 6,
         out_specs=VMEM,
         compiler_params=SMALL,
         name="update_atoms",
-    )(counts, *on_chip(*parts, feats, gain[None, :], w_in, w_out))
+    )(counts, *on_chip(*near, state, gain[None, :], w_in, w_out))
 
 
 def layer(positions, counts, feats, waves, wave_filter, mixing, gain, w_in, w_out):
@@ -395,8 +410,9 @@
     one_behind = (one_behind + from_ahead[1:].astype(f32)).astype(bf16)
     near_behind = shift(one_ahead, 1)
     near_ahead = shift(one_behind, -1)
-    parts = [own, from_ahead, from_behind, opposite, near_behind, near_ahead]
-    return update(counts, parts, feats, gain, w_in, w_out, 1.0 / math.sqrt(kwaves_all))
+    scale = 1.0 / math.sqrt(kwaves_all)
+    state = early_state([own, from_ahead, from_behind, opposite], feats, scale)
+    return update(counts, (near_behind, near_ahead), state, gain, w_in, w_out, scale)
 
 
 def solution(mesh):

time: 90.5 us -> 89.2 us (0.986)
  waiting for transfers between devices: 9.45 us -> 5.69 us
  starting transfers between devices: 37.7 us -> 40.1 us
    ppermute x10, waiting for transfers between devices: 7.81 us -> 4.05 us  [shift(): lax.ppermute(v, 'z', [(i, (i + d) % NZ) for i in range(NZ)])]
    ppermute x10, starting transfers between devices: 30.1 us -> 32.5 us  [shift(): lax.ppermute(v, 'z', [(i, (i + d) % NZ) for i in range(NZ)])]
  transfers between devices with their start and end apart: 13 -> 13, of which waited for: 6 -> 5; matrix products, arithmetic and copies ran while one was open for 0% -> 0% of each run, Pallas kernels for 7% -> 7%
where the time goes in v2:
time: 89.2 us; the launch traced here: 88.4 us
  starting transfers between devices  40.1 us (45%)
  blocking collectives  30.6 us (34%)
  Pallas kernels  11 us (12%)
  waiting for transfers between devices  5.69 us (6%)
    ppermute x10, starting transfers between devices, shift(): lax.ppermute(v, 'z', [(i, (i + d) % NZ) for i in range(NZ)])  32.5 us
    all_to_all x2, blocking collectives, exchange(): return lax.all_to_all(v, ('y', 'x'), 0, 0, tiled=True)  30.6 us
    ppermute x3, starting transfers between devices, partner(): return lax.ppermute(v, 'core', swap)  7.61 us
    ppermute x10, waiting for transfers between devices, shift(): lax.ppermute(v, 'z', [(i, (i + d) % NZ) for i in range(NZ)])  4.05 us
    pallas_call x1, Pallas kernels, early_factors(): pl.pallas_call(kernel, out_shape=(tile, tile, part, part), in_specs=[VMEM...  3.65 us
    pallas_call x2, Pallas kernels, factors(): pl.pallas_call(kernel, out_shape=(pltpu.VMEM((groups, 2, OWN, width), dty...  3.36 us
  transfers between devices with their start and end apart: 13, of which 5 were waited for; matrix products, arithmetic and copies ran while one was open for 0% of the time, Pallas kernels for 7%

profile of v2, /device:TPU:1, one launch (start us, length us, event | category | flops | bytes accessed | tf_op | source)
XLA Modules:
  0.0 88.4 jit_solution(7407993248329957815)
XLA Ops:
  0.7 0.9 pack_atoms.1
  1.5 7.8 %collective-permute-start.3 = (bf16[144,256]{1,0:T(8,128)(2,1)S(1)}, bf16[144,256]{1,0:T(8,128)(2,1)S(1)}, u32[]{:S(2)}, u32[]{:S(2)}) collective-permute-start(bf16[144,256]{1,0:T(8,128)(2,1)S(1)} %get-tuple-element.25.refs_5_), channel_id=1, source_target_pairs={{0,128},{32,160},{64,192},{96,224},{128,0},{160,32},{192,64},{224,... | collective-permute-start | bytes 221192 | tf_op jit(solution)/shard_map/ppermute | solution.py:363
  9.3 1.8 %collective-permute-done.3.refs_4_ = bf16[144,256]{1,0:T(8,128)(2,1)S(1)} collective-permute-done((bf16[144,256]{1,0:T(8,128)(2,1)S(1)}, bf16[144,256]{1,0:T(8,128)(2,1)S(1)}, u32[]{:S(2)}, u32[]{:S(2)}) %collective-permute-start.3) | collective-permute-done | bytes 73760 | tf_op jit(solution)/shard_map/ppermute | solution.py:363
  11.2 4.8 %collective-permute-start.5 = (bf16[288,256]{1,0:T(8,128)(2,1)S(1)}, bf16[288,256]{1,0:T(8,128)(2,1)S(1)}, u32[]{:S(2)}, u32[]{:S(2)}) collective-permute-start(bf16[288,256]{1,0:T(8,128)(2,1)S(1)} %constant_dynamic-update-slice_fusion), channel_id=1, source_target_pairs={{0,224},{32,0},{64,32},{96,64},{128,96},{160,128},{192,160},{224,1... | collective-permute-start | bytes 442376 | tf_op jit(solution)/shard_map/ppermute | solution.py:363
  16.0 0.0 collective-permute-start.4
  16.0 0.0 collective-permute-start.2
  16.0 3.6 %collective-permute-start.1 = (bf16[144,256]{1,0:T(8,128)(2,1)S(1)}, bf16[144,256]{1,0:T(8,128)(2,1)S(1)}, u32[]{:S(2)}, u32[]{:S(2)}) collective-permute-start(bf16[144,256]{1,0:T(8,128)(2,1)S(1)} %get-tuple-element.25.refs_5_), channel_id=1, source_target_pairs={{0,192},{32,224},{64,0},{96,32},{128,64},{160,96},{192,128},{224,1... | collective-permute-start | bytes 221192 | tf_op jit(solution)/shard_map/ppermute | solution.py:363
  19.6 2.0 %collective-permute-start = (bf16[16,512]{1,0:T(8,128)(2,1)S(1)}, bf16[16,512]{1,0:T(8,128)(2,1)S(1)}, u32[]{:S(2)}, u32[]{:S(2)}) collective-permute-start(bf16[16,512]{1,0:T(8,128)(2,1)S(1)} %get-tuple-element.24.refs_1_.refs_0_), channel_id=1, source_target_pairs={{0,1},{1,0},{2,3},{3,2},{4,5},{5,4},{6,7},{7,6},{8,9},{9,8},{10,11... | collective-permute-start | bytes 49160 | tf_op jit(solution)/shard_map/ppermute | solution.py:360
  21.6 0.8 collective-permute-done.refs_0_
  22.4 0.0 collective-permute-done.2.refs_3_
  22.4 0.0 collective-permute-done.1.refs_2_
  22.4 3.6 %early_factors.1 = (bf16[1024,512]{1,0:T(8,128)(2,1)S(1)}, bf16[1024,512]{1,0:T(8,128)(2,1)S(1)}, f32[1024,256]{1,0:T(8,128)S(1)}, f32[1024,256]{1,0:T(8,128)S(1)}) custom-call(bf16[16,512]{1,0:T(8,128)(2,1)S(1)} %collective-permute-done.refs_0_, bf16[16,512]{1,0:T(8,128)(2,1)S(1)} %get-tuple-element.24.refs_1_.refs_0_, ...), custom_call_target="tpu_custom_call" | custom-call | flops 536870912 | bytes 2097152 | tf_op jit(solution)/shard_map/early_factors/pallas_call | solution.py:169
  26.1 0.0 collective-permute-done.5.refs_3_
  26.1 0.0 collective-permute-done.4.refs_2_
  26.1 1.7 %structure_factors.2 = (bf16[16,2,32,256]{3,2,1,0:T(8,128)(2,1)S(1)}, bf16[1024,512]{1,0:T(8,128)(2,1)S(1)}) custom-call(bf16[16,512]{1,0:T(8,128)(2,1)S(1)} %collective-permute-done.refs_0_, f32[1024,256]{1,0:T(8,128)S(1)} %get-tuple-element.27.refs_1_, bf16[288,256]{1,0:T(8,128)(2,1)S(1)} %collective-permute-done.4.refs_2_, ...), custom_call_target="tpu_custom_call" | custom-call | flops 268435456 | bytes 2097152 | tf_op jit(solution)/shard_map/structure_factors/pallas_call | solution.py:204
  27.8 3.4 %collective-permute-start.6 = (bf16[16,2,32,256]{3,2,1,0:T(8,128)(2,1)S(1)}, bf16[16,2,32,256]{3,2,1,0:T(8,128)(2,1)S(1)}, u32[]{:S(2)}, u32[]{:S(2)}) collective-permute-start(bf16[16,2,32,256]{3,2,1,0:T(8,128)(2,1)S(1)} %get-tuple-element.31), channel_id=1, source_target_pairs={{0,1},{1,0},{2,3},{3,2},{4,5},{5,4},{6,7},{7,6},{8,9},{9,8},{10,11... | collective-permute-start | bytes 1572872 | tf_op jit(solution)/shard_map/ppermute | solution.py:360
  31.2 0.0 copy-start.2
  31.2 1.7 %structure_factors.3 = (f32[16,2,32,256]{3,2,1,0:T(8,128)S(1)}, bf16[1024,512]{1,0:T(8,128)(2,1)S(1)}) custom-call(bf16[16,512]{1,0:T(8,128)(2,1)S(1)} %get-tuple-element.24.refs_1_.refs_0_, f32[1024,256]{1,0:T(8,128)S(1)} %get-tuple-element.29.refs_1_, bf16[288,256]{1,0:T(8,128)(2,1)S(1)} %collective-permute-done.4.refs_2_, ...), custom_call_target="tpu_custom_call" | custom-call | flops 268435456 | bytes 2097152 | tf_op jit(solution)/shard_map/structure_factors/pallas_call | solution.py:204
  32.9 0.0 collective-permute-done.6
  32.9 0.2 add_convert_fusion
  33.1 17.1 %all_to_all.10.refs_0_ = bf16[16,2,32,256]{3,2,1,0:T(8,128)(2,1)S(1)} all-to-all(bf16[16,2,32,256]{3,2,1,0:T(8,128)(2,1)S(1)} %add_convert_fusion), channel_id=1, replica_groups=mesh['z'=8,'y'=4,'x'=4,'core'=2] {'y','x'}, dimensions={0} | all-to-all | bytes 1048576 | tf_op jit(solution)/shard_map/all_to_all | solution.py:366
  50.2 0.0 copy-done.2
  50.2 0.4 filter_mix.1
  50.6 13.5 %all_to_all.11.f_ref = bf16[16,2,32,256]{3,2,1,0:T(8,128)(2,1)S(1)} all-to-all(bf16[16,2,32,256]{3,2,1,0:T(8,128)(2,1)S(1)} %filter_mix.1), channel_id=1, replica_groups=mesh['z'=8,'y'=4,'x'=4,'core'=2] {'y','x'}, dimensions={0} | all-to-all | bytes 1048576 | tf_op jit(solution)/shard_map/all_to_all | solution.py:366
  64.1 2.2 %collective-permute-start.7 = (bf16[16,2,32,256]{3,2,1,0:T(8,128)(2,1)S(1)}, bf16[16,2,32,256]{3,2,1,0:T(8,128)(2,1)S(1)}, u32[]{:S(2)}, u32[]{:S(2)}) collective-permute-start(bf16[16,2,32,256]{3,2,1,0:T(8,128)(2,1)S(1)} %all_to_all.11.f_ref), channel_id=1, source_target_pairs={{0,1},{1,0},{2,3},{3,2},{4,5},{5,4},{6,7},{7,6},{8,9},{9,8},{10,11... | collective-permute-start | bytes 1572872 | tf_op jit(solution)/shard_map/ppermute | solution.py:360
  66.2 0.7 own_fields.1
  66.9 0.8 collective-permute-done.7.refs_2_
  67.8 0.0 copy-start.3
  67.8 0.0 copy-start
  67.8 0.0 copy-start.1
  67.8 0.0 copy-start.4
  67.8 0.7 wave_fields.1
  68.5 3.0 %collective-permute-start.8 = (bf16[2,256,128]{2,1,0:T(8,128)(2,1)S(1)}, bf16[2,256,128]{2,1,0:T(8,128)(2,1)S(1)}, u32[]{:S(2)}, u32[]{:S(2)}) collective-permute-start(bf16[2,256,128]{2,1,0:T(8,128)(2,1)S(1)} %get-tuple-element.38), channel_id=1, source_target_pairs={{0,64},{32,96},{64,128},{96,160},{128,192},{160,224},{192,0},{224,... | collective-permute-start | bytes 393224 | tf_op jit(solution)/shard_map/ppermute | solution.py:363
  71.5 1.6 %collective-permute-start.12 = (bf16[1,256,128]{2,1,0:T(8,128)(2,1)S(1)}, bf16[1,256,128]{2,1,0:T(8,128)(2,1)S(1)}, u32[]{:S(2)}, u32[]{:S(2)}) collective-permute-start(bf16[1,256,128]{2,1,0:T(8,128)(2,1)S(1)} %get-tuple-element.42), channel_id=1, source_target_pairs={{0,128},{32,160},{64,192},{96,224},{128,0},{160,32},{192,64},{224,... | collective-permute-start | bytes 196616 | tf_op jit(solution)/shard_map/ppermute | solution.py:363
  73.1 1.8 %collective-permute-start.10 = (bf16[2,256,128]{2,1,0:T(8,128)(2,1)S(1)}, bf16[2,256,128]{2,1,0:T(8,128)(2,1)S(1)}, u32[]{:S(2)}, u32[]{:S(2)}) collective-permute-start(bf16[2,256,128]{2,1,0:T(8,128)(2,1)S(1)} %get-tuple-element.40), channel_id=1, source_target_pairs={{0,192},{32,224},{64,0},{96,32},{128,64},{160,96},{192,128},{224,1... | collective-permute-start | bytes 393224 | tf_op jit(solution)/shard_map/ppermute | solution.py:363
  74.9 1.0 %collective-permute-done.8.refs_2_ = bf16[2,256,128]{2,1,0:T(8,128)(2,1)S(1)} collective-permute-done((bf16[2,256,128]{2,1,0:T(8,128)(2,1)S(1)}, bf16[2,256,128]{2,1,0:T(8,128)(2,1)S(1)}, u32[]{:S(2)}, u32[]{:S(2)}) %collective-permute-start.8) | collective-permute-done | bytes 131104 | tf_op jit(solution)/shard_map/ppermute | solution.py:363
  75.9 7.3 %collective-permute-start.9 = (bf16[1,256,128]{2,1,0:T(8,128)(2,1)S(1)}, bf16[1,256,128]{2,1,0:T(8,128)(2,1)S(1)}, u32[]{:S(2)}, u32[]{:S(2)}) collective-permute-start(bf16[1,256,128]{2,1,0:T(8,128)(2,1)S(1)} %add_convert_fusion.2), channel_id=1, source_target_pairs={{0,32},{32,64},{64,96},{96,128},{128,160},{160,192},{192,224},{224... | collective-permute-start | bytes 196616 | tf_op jit(solution)/shard_map/ppermute | solution.py:363
  83.2 0.0 collective-permute-done.10.refs_1_
  83.2 2.7 %collective-permute-start.11 = (bf16[1,256,128]{2,1,0:T(8,128)(2,1)S(1)}, bf16[1,256,128]{2,1,0:T(8,128)(2,1)S(1)}, u32[]{:S(2)}, u32[]{:S(2)}) collective-permute-start(bf16[1,256,128]{2,1,0:T(8,128)(2,1)S(1)} %add_convert_fusion.1), channel_id=1, source_target_pairs={{0,224},{32,0},{64,32},{96,64},{128,96},{160,128},{192,160},{224,1... | collective-permute-start | bytes 196616 | tf_op jit(solution)/shard_map/ppermute | solution.py:363
  85.9 0.0 collective-permute-done.12.refs_3_
  85.9 0.0 copy-done.3
  85.9 0.1 early_state.1.refs_3_
  86.0 0.0 collective-permute-done.9.refs_1_
  86.0 1.2 %collective-permute-done.11.refs_2_ = bf16[1,256,128]{2,1,0:T(8,128)(2,1)S(1)} collective-permute-done((bf16[1,256,128]{2,1,0:T(8,128)(2,1)S(1)}, bf16[1,256,128]{2,1,0:T(8,128)(2,1)S(1)}, u32[]{:S(2)}, u32[]{:S(2)}) %collective-permute-start.11) | collective-permute-done | bytes 65568 | tf_op jit(solution)/shard_map/ppermute | solution.py:363
  87.2 0.0 copy-done
  87.2 0.0 copy-done.1
  87.2 0.0 copy-done.4
  87.2 1.2 %update_atoms.1 = bf16[128,256]{1,0:T(8,128)(2,1)} custom-call(s32[1]{0:T(128)S(6)} %copy.11.count_ref.refs_0_, bf16[1,256,128]{2,1,0:T(8,128)(2,1)S(1)} %collective-permute-done.9.refs_1_, bf16[1,256,128]{2,1,0:T(8,128)(2,1)S(1)} %collective-permute-done.11.refs_2_, f32[128,256]{1,0:T(8,128)S(1)} %early_state.1.refs_3_, f32[1,256]{1,0:T(1,128)S(1)} %bitcast.3, ...), custom_call_target="tpu_custom_call" | custom-call | tf_op jit(solution)/shard_map/update_atoms/pallas_call | solution.py:339
  (4 shorter events, 0.0 us)
Async XLA Ops:
  1.5 9.7 %collective-permute-start.3 = (bf16[144,256]{1,0:T(8,128)(2,1)S(1)}, bf16[144,256]{1,0:T(8,128)(2,1)S(1)}, u32[]{:S(2)}, u32[]{:S(2)}) collective-permute-start(bf16[144,256]{1,0:T(8,128)(2,1)S(1)} %get-tuple-element.25.refs_5_), channel_id=1, source_target_pairs={{0,128},{32,160},{64,192},{96,224},{128,0},{160,32},{192,64},{224,... | collective-permute-start | bytes 221192 | tf_op jit(solution)/shard_map/ppermute | solution.py:363
  11.2 14.9 %collective-permute-start.5 = (bf16[288,256]{1,0:T(8,128)(2,1)S(1)}, bf16[288,256]{1,0:T(8,128)(2,1)S(1)}, u32[]{:S(2)}, u32[]{:S(2)}) collective-permute-start(bf16[288,256]{1,0:T(8,128)(2,1)S(1)} %constant_dynamic-update-slice_fusion), channel_id=1, source_target_pairs={{0,224},{32,0},{64,32},{96,64},{128,96},{160,128},{192,160},{224,1... | collective-permute-start | bytes 442376 | tf_op jit(solution)/shard_map/ppermute | solution.py:363
  16.0 10.1 %collective-permute-start.4 = (bf16[288,256]{1,0:T(8,128)(2,1)S(1)}, bf16[288,256]{1,0:T(8,128)(2,1)S(1)}, u32[]{:S(2)}, u32[]{:S(2)}) collective-permute-start(bf16[288,256]{1,0:T(8,128)(2,1)S(1)} %constant_dynamic-update-slice_fusion), channel_id=1, source_target_pairs={{0,32},{32,64},{64,96},{96,128},{128,160},{160,192},{192,224},{224... | collective-permute-start | bytes 442376 | tf_op jit(solution)/shard_map/ppermute | solution.py:363
  16.0 6.4 %collective-permute-start.2 = (bf16[144,256]{1,0:T(8,128)(2,1)S(1)}, bf16[144,256]{1,0:T(8,128)(2,1)S(1)}, u32[]{:S(2)}, u32[]{:S(2)}) collective-permute-start(bf16[144,256]{1,0:T(8,128)(2,1)S(1)} %get-tuple-element.25.refs_5_), channel_id=1, source_target_pairs={{0,64},{32,96},{64,128},{96,160},{128,192},{160,224},{192,0},{224,... | collective-permute-start | bytes 221192 | tf_op jit(solution)/shard_map/ppermute | solution.py:363
  16.0 6.4 %collective-permute-start.1 = (bf16[144,256]{1,0:T(8,128)(2,1)S(1)}, bf16[144,256]{1,0:T(8,128)(2,1)S(1)}, u32[]{:S(2)}, u32[]{:S(2)}) collective-permute-start(bf16[144,256]{1,0:T(8,128)(2,1)S(1)} %get-tuple-element.25.refs_5_), channel_id=1, source_target_pairs={{0,192},{32,224},{64,0},{96,32},{128,64},{160,96},{192,128},{224,1... | collective-permute-start | bytes 221192 | tf_op jit(solution)/shard_map/ppermute | solution.py:363
  19.6 2.9 %collective-permute-start = (bf16[16,512]{1,0:T(8,128)(2,1)S(1)}, bf16[16,512]{1,0:T(8,128)(2,1)S(1)}, u32[]{:S(2)}, u32[]{:S(2)}) collective-permute-start(bf16[16,512]{1,0:T(8,128)(2,1)S(1)} %get-tuple-element.24.refs_1_.refs_0_), channel_id=1, source_target_pairs={{0,1},{1,0},{2,3},{3,2},{4,5},{5,4},{6,7},{7,6},{8,9},{9,8},{10,11... | collective-permute-start | bytes 49160 | tf_op jit(solution)/shard_map/ppermute | solution.py:360
  27.8 5.1 %collective-permute-start.6 = (bf16[16,2,32,256]{3,2,1,0:T(8,128)(2,1)S(1)}, bf16[16,2,32,256]{3,2,1,0:T(8,128)(2,1)S(1)}, u32[]{:S(2)}, u32[]{:S(2)}) collective-permute-start(bf16[16,2,32,256]{3,2,1,0:T(8,128)(2,1)S(1)} %get-tuple-element.31), channel_id=1, source_target_pairs={{0,1},{1,0},{2,3},{3,2},{4,5},{5,4},{6,7},{7,6},{8,9},{9,8},{10,11... | collective-permute-start | bytes 1572872 | tf_op jit(solution)/shard_map/ppermute | solution.py:360
  31.2 19.0 %copy-start.2 = (f32[256,256]{1,0:T(8,128)S(1)}, f32[256,256]{1,0:T(8,128)}, u32[]{:S(2)}) copy-start(f32[256,256]{1,0:T(8,128)} %refs_2_.1) | copy-start | bytes 786436
  64.1 3.7 %collective-permute-start.7 = (bf16[16,2,32,256]{3,2,1,0:T(8,128)(2,1)S(1)}, bf16[16,2,32,256]{3,2,1,0:T(8,128)(2,1)S(1)}, u32[]{:S(2)}, u32[]{:S(2)}) collective-permute-start(bf16[16,2,32,256]{3,2,1,0:T(8,128)(2,1)S(1)} %all_to_all.11.f_ref), channel_id=1, source_target_pairs={{0,1},{1,0},{2,3},{3,2},{4,5},{5,4},{6,7},{7,6},{8,9},{9,8},{10,11... | collective-permute-start | bytes 1572872 | tf_op jit(solution)/shard_map/ppermute | solution.py:360
  67.8 18.1 %copy-start.3 = (bf16[128,256]{1,0:T(8,128)(2,1)S(1)}, bf16[128,256]{1,0:T(8,128)(2,1)}, u32[]{:S(2)}) copy-start(bf16[128,256]{1,0:T(8,128)(2,1)} %refs_4_.1) | copy-start | bytes 196612
  67.8 19.5 %copy-start = (bf16[256,1024]{1,0:T(8,128)(2,1)S(1)}, bf16[256,1024]{1,0:T(8,128)(2,1)}, u32[]{:S(2)}) copy-start(bf16[256,1024]{1,0:T(8,128)(2,1)} %refs_5_.1) | copy-start | bytes 1572868
  67.8 19.5 %copy-start.1 = (bf16[1024,256]{1,0:T(8,128)(2,1)S(1)}, bf16[1024,256]{1,0:T(8,128)(2,1)}, u32[]{:S(2)}) copy-start(bf16[1024,256]{1,0:T(8,128)(2,1)} %refs_6_.1) | copy-start | bytes 1572868
  67.8 19.5 %copy-start.4 = (f32[256]{0:T(256)S(1)}, f32[256]{0:T(256)}, u32[]{:S(2)}) copy-start(f32[256]{0:T(256)} %param.15) | copy-start | bytes 3076
  68.5 7.4 %collective-permute-start.8 = (bf16[2,256,128]{2,1,0:T(8,128)(2,1)S(1)}, bf16[2,256,128]{2,1,0:T(8,128)(2,1)S(1)}, u32[]{:S(2)}, u32[]{:S(2)}) collective-permute-start(bf16[2,256,128]{2,1,0:T(8,128)(2,1)S(1)} %get-tuple-element.38), channel_id=1, source_target_pairs={{0,64},{32,96},{64,128},{96,160},{128,192},{160,224},{192,0},{224,... | collective-permute-start | bytes 393224 | tf_op jit(solution)/shard_map/ppermute | solution.py:363
  71.5 14.4 %collective-permute-start.12 = (bf16[1,256,128]{2,1,0:T(8,128)(2,1)S(1)}, bf16[1,256,128]{2,1,0:T(8,128)(2,1)S(1)}, u32[]{:S(2)}, u32[]{:S(2)}) collective-permute-start(bf16[1,256,128]{2,1,0:T(8,128)(2,1)S(1)} %get-tuple-element.42), channel_id=1, source_target_pairs={{0,128},{32,160},{64,192},{96,224},{128,0},{160,32},{192,64},{224,... | collective-permute-start | bytes 196616 | tf_op jit(solution)/shard_map/ppermute | solution.py:363
  73.1 10.0 %collective-permute-start.10 = (bf16[2,256,128]{2,1,0:T(8,128)(2,1)S(1)}, bf16[2,256,128]{2,1,0:T(8,128)(2,1)S(1)}, u32[]{:S(2)}, u32[]{:S(2)}) collective-permute-start(bf16[2,256,128]{2,1,0:T(8,128)(2,1)S(1)} %get-tuple-element.40), channel_id=1, source_target_pairs={{0,192},{32,224},{64,0},{96,32},{128,64},{160,96},{192,128},{224,1... | collective-permute-start | bytes 393224 | tf_op jit(solution)/shard_map/ppermute | solution.py:363
  75.9 10.1 %collective-permute-start.9 = (bf16[1,256,128]{2,1,0:T(8,128)(2,1)S(1)}, bf16[1,256,128]{2,1,0:T(8,128)(2,1)S(1)}, u32[]{:S(2)}, u32[]{:S(2)}) collective-permute-start(bf16[1,256,128]{2,1,0:T(8,128)(2,1)S(1)} %add_convert_fusion.2), channel_id=1, source_target_pairs={{0,32},{32,64},{64,96},{96,128},{128,160},{160,192},{192,224},{224... | collective-permute-start | bytes 196616 | tf_op jit(solution)/shard_map/ppermute | solution.py:363
  83.2 4.0 %collective-permute-start.11 = (bf16[1,256,128]{2,1,0:T(8,128)(2,1)S(1)}, bf16[1,256,128]{2,1,0:T(8,128)(2,1)S(1)}, u32[]{:S(2)}, u32[]{:S(2)}) collective-permute-start(bf16[1,256,128]{2,1,0:T(8,128)(2,1)S(1)} %add_convert_fusion.1), channel_id=1, source_target_pairs={{0,224},{32,0},{64,32},{96,64},{128,96},{160,128},{192,160},{224,1... | collective-permute-start | bytes 196616 | tf_op jit(solution)/shard_map/ppermute | solution.py:363
